TPU v7x, 128 devices: a whole 4x4x4 slice. The times are simulated.
128 devices in a mesh: py: 16 (over y, z_hi, core), px: 8 (over x, z_lo).
Axes of the slice: x: 4, y: 4, z: 4 (z_hi: 2, z_lo: 2; z = z_hi * 2 + z_lo), core: 2. Of those that a mesh axis runs over, the one named last changes fastest.
Arguments:
- frames: float32 [128, 1024, 1024], P(('px', 'py')), may hold values from -6 to 6
- shifts: int32 [128, 2], P(('px', 'py')), may hold values from -8 to 8
- start_basis: float32 [128, 16], replicated, may hold values from -6 to 6
Outputs:
- spatial_components: float32 [16, 1024, 1024], P(None, 'py', 'px')
- temporal_components: float32 [16, 16, 128, 16], P('py', 'px')
- background: float32 [1024, 1024], P('py', 'px')
All inputs are finite; a program needn't handle non-finite values.
Results may differ from a plain program's by a relative error of at most 0.0003.
Values sent between devices are 32-bit elements; how exact they have to be, the bound alone decides.
No kernel may reach another device: no remote copies, remote signals or barrier semaphores. Data moves between devices by JAX's collectives and lax.ppermute only.
A program may use at most 128 MiB of HBM per device.

v0:
```python
import jax
import jax.numpy as jnp
from jax import lax
from jax.experimental import pallas as pl
from jax.experimental.pallas import tpu as pltpu
from jax.sharding import PartitionSpec as P

PATCH = 64
MARGIN = 8
EDGE = PATCH + 2 * MARGIN
RANK = 16
ITERS = 6
SHIFT = 8
SHRINK = 0.5
EPSILON = 1e-06
LANES = 128
REACH = SHIFT + MARGIN
SIDE_ROWS = 40
SHARED_ROWS = 16
SHARED = SIDE_ROWS
FIRST_ROWS = SIDE_ROWS + SHARED_ROWS
CHUNK = 1024
HIGH = lax.Precision.HIGHEST


def lane_ids(shape):
    return lax.broadcasted_iota(jnp.int32, shape, len(shape) - 1)


def spread_kernel(shifts_ref, frame_ref, first_ref, second_ref, padded, sems):
    band = pl.program_id(0)
    height, width = frame_ref.shape
    bands = height // PATCH
    strips = width // LANES

    def rows_in(chunk):
        start = pl.multiple_of(chunk * PATCH, PATCH)
        return pltpu.make_async_copy(
            frame_ref.at[pl.ds(start, PATCH), :],
            padded.at[pl.ds(start + REACH, PATCH), :],
            sems.at[chunk],
        )

    @pl.when(band == 0)
    def _():
        for chunk in range(bands):
            rows_in(chunk).start()
        padded[0:REACH, :] = jnp.zeros((REACH, width), jnp.float32)
        padded[REACH + height :, :] = jnp.zeros((REACH + 8, width), jnp.float32)
        rows_in(0).wait()

    @pl.when(band < bands - 1)
    def _():
        rows_in(band + 1).wait()

    row0 = band * PATCH + MARGIN - shifts_ref[0, 0]
    tile0 = pl.multiple_of(row0 // 8 * 8, 8)
    rest = row0 % 8
    turn = MARGIN + shifts_ref[0, 1]
    lane = lane_ids((EDGE, LANES))
    image_row = lax.broadcasted_iota(jnp.int32, (EDGE, LANES), 0) + (band * PATCH - MARGIN)
    row_ok = (image_row >= 0) & (image_row < height)
    lane_side = lane_ids((SIDE_ROWS, LANES))
    lane_tile = lane_ids((8, LANES))

    kept = lax.broadcasted_iota(jnp.int32, (8, LANES), 0) < 8 - rest

    def turned(strip):
        rows = padded[pl.ds(tile0, EDGE + 8), strip * LANES : (strip + 1) * LANES]
        tiles = [pltpu.roll(rows[at : at + 8], 8 - rest, 0) for at in range(0, EDGE + 8, 8)]
        rows = jnp.concatenate(
            [jnp.where(kept, tile, below) for tile, below in zip(tiles, tiles[1:])], axis=0
        )
        rows = jnp.where(row_ok, rows, 0.0)
        return pltpu.roll(rows, turn, 1)

    late = lane >= turn
    before = turned(0)
    here = jnp.where(late & (lane >= MARGIN), before, 0.0)
    for strip in range(strips):
        if strip + 1 < strips:
            following = turned(strip + 1)
            after = jnp.where(late, following, before)
            before = following
        else:
            after = jnp.where(late | (lane >= MARGIN), 0.0, before)
        first_ref[strip, 0, 0:SIDE_ROWS, :] = jnp.where(
            lane_side < PATCH, here[:SIDE_ROWS], pltpu.roll(here[SIDE_ROWS:], PATCH, 1)
        )
        for tile, groups in ((0, range(8)), (1, range(8, 10))):
            packed = jnp.zeros((8, LANES), jnp.float32)
            for slot, group in enumerate(groups):
                part = here[8 * group : 8 * group + 8]
                part = pltpu.roll(part, (16 * slot - PATCH) % LANES, 1)
                inside = (lane_tile >= 16 * slot) & (lane_tile < 16 * slot + 16)
                packed = jnp.where(inside, part, packed)
            first_ref[strip, 0, SHARED + 8 * tile : SHARED + 8 * tile + 8, :] = packed
        joined = jnp.where(lane < 16, after, here)
        second_ref[strip, 0, :, :] = jnp.where(
            lane_side < PATCH,
            pltpu.roll(joined[:SIDE_ROWS], 48, 1),
            pltpu.roll(joined[SIDE_ROWS:], 112, 1),
        )
        here = after


def spread(frame, shifts, n_rows, n_cols):
    height, width = frame.shape
    shape = lambda rows: jax.ShapeDtypeStruct((n_cols, n_rows, rows, LANES), jnp.float32)
    block = lambda rows: pl.BlockSpec((n_cols, 1, rows, LANES), lambda band: (0, band, 0, 0))
    first, second = pl.pallas_call(
        spread_kernel,
        grid=(n_rows,),
        out_shape=(shape(FIRST_ROWS), shape(SIDE_ROWS)),
        in_specs=[pl.BlockSpec(memory_space=pltpu.SMEM), pl.BlockSpec(memory_space=pl.ANY)],
        out_specs=(block(FIRST_ROWS), block(SIDE_ROWS)),
        scratch_shapes=[
            pltpu.VMEM((height + 2 * REACH + 8, width), jnp.float32),
            pltpu.SemaphoreType.DMA((height // PATCH,)),
        ],
        compiler_params=pltpu.CompilerParams(vmem_limit_bytes=24 << 20),
        name="spread",
    )(shifts, frame)
    peers = n_rows * n_cols
    return (
        first.reshape(peers, FIRST_ROWS, LANES),
        second.reshape(peers, SIDE_ROWS, LANES),
    )


def split(values):
    high = values.astype(jnp.bfloat16)
    low = (values - high.astype(jnp.float32)).astype(jnp.bfloat16)
    return high, low


def eliminate(gram, rows):
    count, width = rows.shape
    half = count // 2
    column = [jnp.broadcast_to(gram[:, k : k + 1], (count, width)) for k in range(count)]
    upper = [c[:half] for c in column]
    lower = [c[half:] for c in column]
    row_id = lax.broadcasted_iota(jnp.int32, (half, width), 0)
    top, bottom = rows[:half], rows[half:]
    for j in range(count):
        at = j % half
        source = upper[j] if j < half else lower[j]
        pivot = source[at : at + 1]
        inverse = 1.0 / pivot
        root = lax.rsqrt(pivot)
        below = lower[j] * inverse
        if j < half:
            side = upper[j] * inverse
            for k in range(j + 1, half):
                entry = upper[j][k : k + 1]
                upper[k] = upper[k] - side * entry
                lower[k] = lower[k] - below * entry
            for k in range(half, count):
                lower[k] = lower[k] - below * lower[j][k - half : k - half + 1]
            pivot_row = top[at : at + 1]
            change = jnp.where(row_id > at, top - side * pivot_row, top)
            top = jnp.where(row_id == at, top * root, change)
            bottom = bottom - below * pivot_row
        else:
            for k in range(j + 1, count):
                lower[k] = lower[k] - below * lower[j][k - half : k - half + 1]
            pivot_row = bottom[at : at + 1]
            change = jnp.where(row_id > at, bottom - below * pivot_row, bottom)
            bottom = jnp.where(row_id == at, bottom * root, change)
    return jnp.concatenate([top, bottom], axis=0)


def orthonormal_rows(rows):
    count = rows.shape[0]
    across = lax.broadcasted_iota(jnp.int32, (count, count), 0)
    ident = jnp.where(across == lane_ids((count, count)), EPSILON, 0.0)
    for sweep in range(2):
        gram = lax.dot_general(
            rows, rows, (((1,), (1,)), ((), ())), precision=HIGH, preferred_element_type=jnp.float32
        )
        rows = eliminate(gram + ident, rows)
    return rows


def orth_kernel(start_ref, out_ref):
    out_ref[...] = orthonormal_rows(start_ref[...])


def start_rows(start):
    return pl.pallas_call(
        orth_kernel,
        out_shape=jax.ShapeDtypeStruct(start.shape, jnp.float32),
        in_specs=[pl.BlockSpec(memory_space=pltpu.VMEM)],
        out_specs=pl.BlockSpec(memory_space=pltpu.VMEM),
        name="start_rows",
    )(start)


def place_inner(tiles, patch):
    lane = lane_ids((8, LANES))
    placed = []
    for group in range(1, 9):
        turn = (-MARGIN if patch == 0 else PATCH + MARGIN) - (0 if group < 5 else PATCH)
        own = pltpu.roll(tiles[group % 5], turn % LANES, 1)
        strip = tiles[5 + group // 8]
        both = pltpu.roll(strip, (56 - 16 * (group % 8)) % LANES, 1)
        from_own = lane < PATCH - MARGIN if patch == 0 else lane >= PATCH + MARGIN
        placed.append(jnp.where(from_own, own, both))
    return placed


def patch_kernel(patch, *refs):
    if patch == 0:
        first_ref, start_ref, spatial_ref, mean_ref, basis_ref = refs[:5]
        earlier = None
        blocks = [(first_ref, g) for g in range(7)]
    else:
        second_ref, first_ref, start_ref = refs[:3]
        earlier = refs[3:6]
        spatial_ref, mean_ref, basis_ref = refs[6:9]
        blocks = [(second_ref, g) for g in range(5)] + [(first_ref, g) for g in (5, 6)]
    raw, movie, projected, packed, sems = refs[-5:]
    frames = raw.shape[1] // 8
    tiles = len(blocks)
    pixels = tiles * 8 * LANES
    copies = []
    for i, (ref, g) in enumerate(blocks):
        copies.append(
            pltpu.make_async_copy(
                ref.at[:, 8 * g : 8 * g + 8, :],
                raw.at[i].reshape(frames, 8, LANES),
                sems.at[i],
            )
        )
        copies[-1].start()
    means = []
    for i in range(tiles):
        copies[i].wait()

        @pl.loop(0, 8)
        def _(s, i=i):
            values = raw[i, pl.ds(s, frames, stride=8), :]
            mean = jnp.sum(values, axis=0, keepdims=True) * (1.0 / frames)
            packed[pl.ds(8 * i + s, 1), :] = mean
            high, low = split(values - mean)
            lanes = pl.ds(pl.multiple_of((8 * i + s) * LANES, LANES), LANES)
            movie[0:frames, lanes] = high
            movie[frames:, lanes] = low

    mean_tiles = [packed[8 * i : 8 * i + 8, :] for i in range(tiles)]
    keep = lane_ids((8, LANES)) < PATCH
    placed = place_inner(mean_tiles, patch)
    for group in range(8):
        value = placed[group]
        if patch == 1:
            value = jnp.where(keep, earlier[1][8 * group : 8 * group + 8, :], value)
        mean_ref[8 * group : 8 * group + 8, :] = value

    def project(basis):
        high, low = split(basis)
        left = jnp.concatenate(
            [jnp.concatenate([high, high], axis=1), jnp.concatenate([low, low], axis=1)], axis=0
        )
        total = jnp.zeros((RANK, LANES), jnp.float32)
        for start in range(0, pixels, CHUNK):
            both = jnp.dot(
                left, movie[:, start : start + CHUNK], preferred_element_type=jnp.float32
            )
            value = both[:RANK] + both[RANK:]
            projected[:, start : start + CHUNK] = value
            for k in range(0, CHUNK, LANES):
                piece = value[:, k : k + LANES]
                total = total + piece * piece
        mean_square = jnp.sum(total, axis=1, keepdims=True) * (1.0 / (EDGE * EDGE))
        return SHRINK * jnp.sqrt(mean_square + EPSILON)

    def shrunk(value, level):
        return value - jnp.clip(value, -level, level)

    def update(level):
        total = jnp.zeros((2 * RANK, 2 * frames), jnp.float32)
        for start in range(0, pixels, CHUNK):
            factor = shrunk(projected[:, start : start + CHUNK], level)
            left = jnp.concatenate(split(factor), axis=0)
            total = total + lax.dot_general(
                left,
                movie[:, start : start + CHUNK],
                (((1,), (1,)), ((), ())),
                preferred_element_type=jnp.float32,
            )
        total = total[:RANK] + total[RANK:]
        return total[:, :frames] + total[:, frames:]

    basis = lax.fori_loop(
        0, ITERS, lambda _, rows: orthonormal_rows(update(project(rows))), start_ref[...]
    )
    level = project(basis)
    for row in range(tiles * 8):
        packed[pl.ds(row, RANK, stride=tiles * 8), :] = shrunk(
            projected[:, row * LANES : (row + 1) * LANES], level
        )
    for part in range(RANK):
        base = part * tiles * 8
        placed = place_inner([packed[base + 8 * i : base + 8 * i + 8, :] for i in range(tiles)], patch)
        for group in range(8):
            value = placed[group]
            if patch == 1:
                value = jnp.where(keep, earlier[0][part, 8 * group : 8 * group + 8, :], value)
            spatial_ref[part, 8 * group : 8 * group + 8, :] = value
    scaled = basis * jnp.sqrt(jnp.float32(frames))
    square = jnp.concatenate([scaled, jnp.zeros((frames - RANK, frames), jnp.float32)], axis=0)
    turned = square.T[:, :RANK]
    if patch == 0:
        basis_ref[...] = turned
    else:
        basis_ref[0] = earlier[2][...]
        basis_ref[1] = turned


def decompose(patch, *operands):
    frames = operands[0].shape[0]
    tiles = FIRST_ROWS // 8
    pixels = FIRST_ROWS * LANES
    vmem = pl.BlockSpec(memory_space=pltpu.VMEM)
    whole = pl.BlockSpec(memory_space=pl.ANY)
    bases = (frames, RANK) if patch == 0 else (2, frames, RANK)
    in_specs = [whole, vmem] if patch == 0 else [whole, whole, vmem, vmem, vmem, vmem]
    return pl.pallas_call(
        lambda *refs: patch_kernel(patch, *refs),
        out_shape=(
            jax.ShapeDtypeStruct((RANK, PATCH, LANES), jnp.float32),
            jax.ShapeDtypeStruct((PATCH, LANES), jnp.float32),
            jax.ShapeDtypeStruct(bases, jnp.float32),
        ),
        in_specs=in_specs,
        out_specs=(vmem, vmem, vmem),
        scratch_shapes=[
            pltpu.VMEM((tiles, frames * 8, LANES), jnp.float32),
            pltpu.VMEM((2 * frames, pixels), jnp.bfloat16),
            pltpu.VMEM((RANK, pixels), jnp.float32),
            pltpu.VMEM((RANK * FIRST_ROWS, LANES), jnp.float32),
            pltpu.SemaphoreType.DMA((tiles,)),
        ],
        compiler_params=pltpu.CompilerParams(vmem_limit_bytes=32 << 20),
        cost_estimate=pl.CostEstimate(
            flops=26 * 64 * 256 * pixels, bytes_accessed=4 * frames * pixels, transcendentals=0
        ),
        name="patch_0" if patch == 0 else "patch_1",
    )(*operands)


def on_device(frames, shifts, start_basis):
    n_rows = lax.axis_size("py")
    n_cols = lax.axis_size("px")
    first, second = spread(frames[0], shifts, n_rows, n_cols)
    first = lax.all_to_all(first, ("px", "py"), split_axis=0, concat_axis=0, tiled=True)
    second = lax.all_to_all(second, ("px", "py"), split_axis=0, concat_axis=0, tiled=True)
    start = start_rows(start_basis.T)
    left = decompose(0, first, start)
    spatial, background, bases = decompose(1, second, first, start, *left)
    return (spatial, bases[None], background)


def solution(mesh):
    placed = (P(("px", "py"), None, None), P(("px", "py"), None), P())
    return jax.shard_map(
        on_device,
        mesh=mesh,
        in_specs=placed,
        out_specs=(P(None, "py", "px"), P("py", "px", None, None), P("py", "px")),
        check_vma=False,
    )
```

profile of v0, /device:TPU:1, one launch (start us, length us, event | category | flops | bytes accessed | tf_op | source)
XLA Modules:
  0.0 137.0 jit_solution(12480977320170651729)
XLA Ops:
  0.6 0.0 copy-start
  0.6 2.2 %copy-done = f32[1,1024,1024]{2,1,0:T(8,128)S(1)} copy-done((f32[1,1024,1024]{2,1,0:T(8,128)S(1)}, f32[1,1024,1024]{2,1,0:T(8,128)}, u32[]{:S(2)}) %copy-start) | copy-done | bytes 4194328
  2.8 0.0 copy-start.6
  2.8 0.7 copy-done.6
  3.5 10.6 %spread.1 = (f32[8,16,56,128]{3,2,1,0:T(8,128)S(1)}, f32[8,16,40,128]{3,2,1,0:T(8,128)S(1)}) custom-call(s32[1,2]{1,0:T(1,128)S(1)} %copy-done.6, f32[1024,1024]{1,0:T(8,128)S(1)} %bitcast.5), custom_call_target="tpu_custom_call" | custom-call | tf_op jit(solution)/shard_map/spread/pallas_call | solution.py:111
  14.0 0.0 copy-start.3
  14.1 58.2 %all_to_all.10.refs_0_.refs_1_ = f32[128,56,128]{2,1,0:T(8,128)} all-to-all(f32[128,56,128]{2,1,0:T(8,128)S(1)} %bitcast.6), channel_id=1, replica_groups=mesh['py'=16,'px'=8] {'px','py'}, dimensions={0} | all-to-all | bytes 7340032 | tf_op jit(solution)/shard_map/all_to_all | solution.py:356
  72.3 0.0 copy-done.3
  72.3 5.5 %all-to-all-start = ((f32[128,40,128]{2,1,0:T(8,128)}), f32[128,40,128]{2,1,0:T(8,128)S(1)}, u32[]{:S(2)}, u32[]{:S(2)}) async-start(f32[128,40,128]{2,1,0:T(8,128)} %bitcast.7), calls=%async_computation | async-start | bytes 5242880 | tf_op jit(solution)/shard_map/all_to_all | solution.py:357
  77.7 2.0 %start_rows.1.refs_1_.refs_2_ = f32[16,128]{1,0:T(8,128)} custom-call(f32[16,128]{1,0:T(8,128)} %bitcast.9), custom_call_target="tpu_custom_call" | custom-call | tf_op jit(solution)/shard_map/start_rows/pallas_call | solution.py:190
  79.8 0.0 copy-start.1
  79.8 2.0 %copy-done.1 = f32[128,56,128]{2,1,0:T(8,128)S(1)} copy-done((f32[128,56,128]{2,1,0:T(8,128)S(1)}, f32[128,56,128]{2,1,0:T(8,128)}, u32[]{:S(2)}) %copy-start.1) | copy-done | bytes 3670040
  81.8 0.0 copy-start.4
  81.8 0.7 copy-done.4
  82.5 0.0 copy-start.5
  82.5 20.9 %patch_0.1 = (f32[16,64,128]{2,1,0:T(8,128)S(1)}, f32[64,128]{1,0:T(8,128)S(1)}, f32[128,16]{1,0:T(8,128)S(1)}) custom-call(f32[128,56,128]{2,1,0:T(8,128)S(1)} %copy-done.1, f32[16,128]{1,0:T(8,128)S(1)} %copy-done.4), custom_call_target="tpu_custom_call" | custom-call | flops 3053453312 | bytes 3670016 | tf_op jit(solution)/shard_map/patch_0/pallas_call | solution.py:328
  103.4 9.2 %all-to-all-done.refs_0_ = f32[128,40,128]{2,1,0:T(8,128)S(1)} async-done(((f32[128,40,128]{2,1,0:T(8,128)}), f32[128,40,128]{2,1,0:T(8,128)S(1)}, u32[]{:S(2)}, u32[]{:S(2)}) %all-to-all-start) | async-done | bytes 2621472 | tf_op jit(solution)/shard_map/all_to_all | solution.py:357
  112.7 0.0 copy-done.5
  112.7 0.0 copy-start.2
  112.7 2.0 %copy-done.2 = f32[128,56,128]{2,1,0:T(8,128)S(1)} copy-done((f32[128,56,128]{2,1,0:T(8,128)S(1)}, f32[128,56,128]{2,1,0:T(8,128)}, u32[]{:S(2)}) %copy-start.2) | copy-done | bytes 3670040
  114.7 21.6 %patch_1.1 = (f32[16,64,128]{2,1,0:T(8,128)}, f32[64,128]{1,0:T(8,128)}, f32[2,128,16]{2,1,0:T(8,128)S(1)}) custom-call(f32[128,40,128]{2,1,0:T(8,128)S(1)} %all-to-all-done.refs_0_, f32[128,56,128]{2,1,0:T(8,128)S(1)} %copy-done.2, f32[16,128]{1,0:T(8,128)S(1)} %copy-done.5, f32[16,64,128]{2,1,0:T(8,128)S(1)} %get-tuple-element.13.refs_3_, ...), custom_call_target="tpu_custom_call" | custom-call | flops 3053453312 | bytes 3670016 | tf_op jit(solution)/shard_map/patch_1/pallas_call | solution.py:328
  136.4 0.7 copy.6
Async XLA Ops:
  0.6 2.2 %copy-start = (f32[1,1024,1024]{2,1,0:T(8,128)S(1)}, f32[1,1024,1024]{2,1,0:T(8,128)}, u32[]{:S(2)}) copy-start(f32[1,1024,1024]{2,1,0:T(8,128)} %param.3) | copy-start | bytes 12582916
  2.8 0.7 copy-start.6
  14.0 58.2 %copy-start.3 = (f32[8,16,40,128]{3,2,1,0:T(8,128)}, f32[8,16,40,128]{3,2,1,0:T(8,128)S(1)}, u32[]{:S(2)}) copy-start(f32[8,16,40,128]{3,2,1,0:T(8,128)S(1)} %get-tuple-element.11) | copy-start | bytes 7864324
  72.3 40.4 %all-to-all-start = ((f32[128,40,128]{2,1,0:T(8,128)}), f32[128,40,128]{2,1,0:T(8,128)S(1)}, u32[]{:S(2)}, u32[]{:S(2)}) async-start(f32[128,40,128]{2,1,0:T(8,128)} %bitcast.7), calls=%async_computation | async-start | bytes 5242880 | tf_op jit(solution)/shard_map/all_to_all | solution.py:357
  79.8 2.0 %copy-start.1 = (f32[128,56,128]{2,1,0:T(8,128)S(1)}, f32[128,56,128]{2,1,0:T(8,128)}, u32[]{:S(2)}) copy-start(f32[128,56,128]{2,1,0:T(8,128)} %all_to_all.10.refs_0_.refs_1_) | copy-start | bytes 11010052
  81.8 0.7 copy-start.4
  82.5 30.1 %copy-start.5 = (f32[16,128]{1,0:T(8,128)S(1)}, f32[16,128]{1,0:T(8,128)}, u32[]{:S(2)}) copy-start(f32[16,128]{1,0:T(8,128)} %start_rows.1.refs_1_.refs_2_) | copy-start | bytes 24580
  112.7 2.0 %copy-start.2 = (f32[128,56,128]{2,1,0:T(8,128)S(1)}, f32[128,56,128]{2,1,0:T(8,128)}, u32[]{:S(2)}) copy-start(f32[128,56,128]{2,1,0:T(8,128)} %all_to_all.10.refs_0_.refs_1_) | copy-start | bytes 11010052
where the time goes:
time: 137 us
  blocking collectives  58.2 us (42%)
  Pallas kernels  55.2 us (40%)
  waiting for transfers between devices  9.23 us (7%)
  local copies, waits for them, and re-layouts  8.29 us (6%)
  starting transfers between devices  5.48 us (4%)
    all_to_all x1, blocking collectives, on_device(): lax.all_to_all(first, ('px', 'py'), split_axis=0, concat_axis=0, tiled=True)  58.2 us
    pallas_call x2, Pallas kernels, decompose(): pl.pallas_call(lambda *refs: patch_kernel(patch, *refs), out_shape=(jax.S...  42.5 us
    pallas_call x1, Pallas kernels, spread(): pl.pallas_call(spread_kernel, grid=(n_rows,), out_shape=(shape(FIRST_ROWS...  10.6 us
    all_to_all x1, waiting for transfers between devices, on_device(): lax.all_to_all(second, ('px', 'py'), split_axis=0, concat_axis=0, tiled=T...  9.23 us
    unnamed x15, local copies, waits for them, and re-layouts  8.29 us
    all_to_all x1, starting transfers between devices, on_device(): lax.all_to_all(second, ('px', 'py'), split_axis=0, concat_axis=0, tiled=T...  5.48 us
  transfers between devices with their start and end apart: 1, of which 1 were waited for; matrix products, arithmetic and copies ran while one was open for 0% of the time, Pallas kernels for 17%

commit v1 on v0

v1 whole, which is shorter than its diff:
```python
import jax
import jax.numpy as jnp
from jax import lax
from jax.experimental import pallas as pl
from jax.experimental.pallas import tpu as pltpu
from jax.sharding import PartitionSpec as P

PATCH = 64
MARGIN = 8
EDGE = PATCH + 2 * MARGIN
RANK = 16
ITERS = 6
SHIFT = 8
SHRINK = 0.5
EPSILON = 1e-06
LANES = 128
REACH = SHIFT + MARGIN
GROUP = 8
HALF = 64
SHARED = 16
FIRST_ROWS = 48
SECOND_ROWS = 32
HIGH = lax.Precision.HIGHEST


def lane_ids(shape):
    return lax.broadcasted_iota(jnp.int32, shape, len(shape) - 1)


def spread_kernel(shifts_hbm, frame_ref, first_ref, second_ref, padded, shifts_ref, sems, shift_sem):
    band = pl.program_id(0)
    height, width = frame_ref.shape
    bands = height // PATCH
    strips = width // LANES

    def rows_in(chunk):
        start = pl.multiple_of(chunk * PATCH, PATCH)
        return pltpu.make_async_copy(
            frame_ref.at[pl.ds(start, PATCH), :],
            padded.at[pl.ds(start + REACH, PATCH), :],
            sems.at[chunk],
        )

    @pl.when(band == 0)
    def _():
        shift_copy = pltpu.make_async_copy(shifts_hbm, shifts_ref, shift_sem)
        shift_copy.start()
        for chunk in range(bands):
            rows_in(chunk).start()
        padded[0:REACH, :] = jnp.zeros((REACH, width), jnp.float32)
        padded[REACH + height :, :] = jnp.zeros((REACH + GROUP, width), jnp.float32)
        shift_copy.wait()
        rows_in(0).wait()

    @pl.when(band < bands - 1)
    def _():
        rows_in(band + 1).wait()

    odd = band % 2
    row0 = band * PATCH + MARGIN * (1 + odd) - shifts_ref[0, 0]
    tile0 = row0 // GROUP * GROUP
    rest = row0 % GROUP
    starts = [
        pl.multiple_of(tile0 + GROUP * jnp.where(odd == 0, p, 8 - p), GROUP) for p in range(9)
    ]
    margin_inside = (band > 0) & (band < bands - 1)
    margin_inside = margin_inside.astype(jnp.int32)
    turn = MARGIN + shifts_ref[0, 1]
    shape = (GROUP, LANES)
    lane = lane_ids(shape)
    lower = lane < HALF
    from_above = lax.broadcasted_iota(jnp.int32, shape, 0) >= rest
    from_here = lane < LANES - turn
    landing = (lane + turn) % LANES
    to_next = landing < 16
    zeros = jnp.zeros(shape, jnp.float32)

    def rows_of(strip):
        lanes = slice(strip * LANES, (strip + 1) * LANES)
        tiles = []
        for p in range(9):
            pair = padded[pl.ds(starts[p], 2 * GROUP), lanes]
            tile = jnp.where(from_above, pair[:GROUP], pair[GROUP:])
            tile = pltpu.roll(tile, GROUP - rest, 0)
            if p == 0:
                tile = jnp.where(margin_inside > 0, tile, 0.0)
            tiles.append(tile)
        return tiles

    def rolled(tile, amount):
        return pltpu.roll(tile, (turn + amount) % LANES, 1)

    before = rows_of(0)
    here = [jnp.where(from_here & (landing >= MARGIN), tile, 0.0) for tile in before]
    for strip in range(strips):
        if strip + 1 < strips:
            following = rows_of(strip + 1)
            after = [jnp.where(from_here, n, b) for n, b in zip(following, before)]
            before = following
        else:
            after = [jnp.where(from_here | (landing >= MARGIN), 0.0, b) for b in before]
        joined = [jnp.where(to_next, a, h) for a, h in zip(after, here)]
        tile = rolled(here[8], 0)
        for p in (1, 2, 3):
            tile = jnp.where(lane >= HALF + SHARED * p, rolled(here[p], SHARED * p), tile)
        first_ref[strip, 0, 0:8, :] = tile
        tile = rolled(joined[8], 48)
        for p in (4, 5, 6, 7):
            tile = jnp.where(lane >= SHARED * p, rolled(here[p], SHARED * (p - 4)), tile)
        first_ref[strip, 0, 8:16, :] = tile
        for i in range(4):
            rows = slice(GROUP * i, GROUP * i + GROUP)
            first_ref[strip, 0, 16 + GROUP * i : 24 + GROUP * i, :] = jnp.where(
                lower, rolled(here[i], 0), rolled(here[i + 4], HALF)
            )
            second_ref[strip, 0, rows, :] = jnp.where(
                lower, rolled(joined[i], 48), rolled(joined[i + 4], 112)
            )
        here = after


def spread(frame, shifts, n_rows, n_cols):
    height, width = frame.shape
    shape = lambda rows: jax.ShapeDtypeStruct((n_cols, n_rows, rows, LANES), jnp.float32)
    block = lambda rows: pl.BlockSpec((n_cols, 1, rows, LANES), lambda band: (0, band, 0, 0))
    first, second = pl.pallas_call(
        spread_kernel,
        grid=(n_rows,),
        out_shape=(shape(FIRST_ROWS), shape(SECOND_ROWS)),
        in_specs=[pl.BlockSpec(memory_space=pltpu.HBM), pl.BlockSpec(memory_space=pltpu.HBM)],
        out_specs=(block(FIRST_ROWS), block(SECOND_ROWS)),
        scratch_shapes=[
            pltpu.VMEM((height + 2 * REACH + GROUP, width), jnp.float32),
            pltpu.SMEM(shifts.shape, jnp.int32),
            pltpu.SemaphoreType.DMA((height // PATCH,)),
            pltpu.SemaphoreType.DMA,
        ],
        compiler_params=pltpu.CompilerParams(vmem_limit_bytes=24 << 20),
        name="spread",
    )(shifts, frame)
    peers = n_rows * n_cols
    return (
        first.reshape(peers, FIRST_ROWS, LANES),
        second.reshape(peers, SECOND_ROWS, LANES),
    )


def tile_copy(source, group, target, sem):
    frames = source.shape[0]
    return pltpu.make_async_copy(
        source.at[:, GROUP * group : GROUP * group + GROUP, :],
        target.reshape(frames, GROUP, LANES),
        sem,
    )


def narrow_rows(tiles, lane0):
    frames = tiles.shape[0] // GROUP
    lane = lane_ids((frames, LANES))
    row = jnp.zeros((frames, LANES), jnp.float32)
    for s in range(GROUP):
        values = tiles[pl.ds(s, frames, stride=GROUP), :]
        values = pltpu.roll(values, (SHARED * s - lane0) % LANES, 1)
        row = jnp.where(lane >= SHARED * s, values, row)
    return row


def pack_kernel(first_ref, edge_ref, far_ref, tile, sems):
    frames = first_ref.shape[0]
    whole = pltpu.make_async_copy(first_ref.at[:, 0 : 2 * GROUP, :], edge_ref, sems.at[0])
    whole.start()
    copy = tile_copy(first_ref, 0, tile, sems.at[1])
    copy.start()
    copy.wait()
    far_ref[...] = narrow_rows(tile, HALF + SHARED)
    whole.wait()


def pack(first):
    frames = first.shape[0]
    return pl.pallas_call(
        pack_kernel,
        out_shape=(
            jax.ShapeDtypeStruct((frames, 2 * GROUP, LANES), jnp.float32),
            jax.ShapeDtypeStruct((frames, LANES), jnp.float32),
        ),
        in_specs=[pl.BlockSpec(memory_space=pltpu.HBM)],
        out_specs=(
            pl.BlockSpec(memory_space=pltpu.HBM),
            pl.BlockSpec(memory_space=pltpu.VMEM),
        ),
        scratch_shapes=[
            pltpu.VMEM((frames * GROUP, LANES), jnp.float32),
            pltpu.SemaphoreType.DMA((2,)),
        ],
        name="pack",
    )(first)


def split(values):
    high = values.astype(jnp.bfloat16)
    low = (values - high.astype(jnp.float32)).astype(jnp.bfloat16)
    return high, low


def eliminate(gram, rows):
    count, width = rows.shape
    half = count // 2
    column = [jnp.broadcast_to(gram[:, k : k + 1], (count, width)) for k in range(count)]
    upper = [c[:half] for c in column]
    lower = [c[half:] for c in column]
    row_id = lax.broadcasted_iota(jnp.int32, (half, width), 0)
    top, bottom = rows[:half], rows[half:]
    for j in range(count):
        at = j % half
        source = upper[j] if j < half else lower[j]
        pivot = source[at : at + 1]
        inverse = 1.0 / pivot
        root = lax.rsqrt(pivot)
        below = lower[j] * inverse
        if j < half:
            side = upper[j] * inverse
            for k in range(j + 1, half):
                entry = upper[j][k : k + 1]
                upper[k] = upper[k] - side * entry
                lower[k] = lower[k] - below * entry
            for k in range(half, count):
                lower[k] = lower[k] - below * lower[j][k - half : k - half + 1]
            pivot_row = top[at : at + 1]
            change = jnp.where(row_id > at, top - side * pivot_row, top)
            top = jnp.where(row_id == at, top * root, change)
            bottom = bottom - below * pivot_row
        else:
            for k in range(j + 1, count):
                lower[k] = lower[k] - below * lower[j][k - half : k - half + 1]
            pivot_row = bottom[at : at + 1]
            change = jnp.where(row_id > at, bottom - below * pivot_row, bottom)
            bottom = jnp.where(row_id == at, bottom * root, change)
    return jnp.concatenate([top, bottom], axis=0)


def orthonormal_rows(rows):
    count = rows.shape[0]
    across = lax.broadcasted_iota(jnp.int32, (count, count), 0)
    ident = jnp.where(across == lane_ids((count, count)), EPSILON, 0.0)
    for sweep in range(2):
        gram = lax.dot_general(
            rows, rows, (((1,), (1,)), ((), ())), precision=HIGH, preferred_element_type=jnp.float32
        )
        rows = eliminate(gram + ident, rows)
    return rows


def orth_kernel(start_ref, out_ref):
    out_ref[...] = orthonormal_rows(start_ref[...])


def start_rows(start):
    return pl.pallas_call(
        orth_kernel,
        out_shape=jax.ShapeDtypeStruct(start.shape, jnp.float32),
        in_specs=[pl.BlockSpec(memory_space=pltpu.VMEM)],
        out_specs=pl.BlockSpec(memory_space=pltpu.VMEM),
        name="start_rows",
    )(start)


def centred(values):
    frames = values.shape[0]
    mean = jnp.sum(values, axis=0, keepdims=True) * (1.0 / frames)
    return mean, split(values - mean)


def keep_row(row, values, movie, means):
    frames = values.shape[0]
    mean, (high, low) = centred(values)
    means[pl.ds(row, 1), :] = mean
    lanes = pl.ds(pl.multiple_of(row * LANES, LANES), LANES)
    movie[0:frames, lanes] = high
    movie[frames:, lanes] = low


def iterate(basis, chunks, projected, frames):
    def project(basis):
        high, low = split(basis)
        left = jnp.concatenate(
            [jnp.concatenate([high, high], axis=1), jnp.concatenate([low, low], axis=1)], axis=0
        )
        total = jnp.zeros((RANK, LANES), jnp.float32)
        for movie, start, width, here in chunks:
            both = jnp.dot(
                left, movie[:, start : start + width], preferred_element_type=jnp.float32
            )
            value = both[:RANK] + both[RANK:]
            projected[:, here : here + width] = value
            for k in range(0, width, LANES):
                piece = value[:, k : k + LANES]
                total = total + piece * piece
        mean_square = jnp.sum(total, axis=1, keepdims=True) * (1.0 / (EDGE * EDGE))
        return SHRINK * jnp.sqrt(mean_square + EPSILON)

    def update(level):
        total = jnp.zeros((2 * RANK, 2 * frames), jnp.float32)
        for movie, start, width, here in chunks:
            factor = shrunk(projected[:, here : here + width], level)
            left = jnp.concatenate(split(factor), axis=0)
            total = total + lax.dot_general(
                left,
                movie[:, start : start + width],
                (((1,), (1,)), ((), ())),
                preferred_element_type=jnp.float32,
            )
        total = total[:RANK] + total[RANK:]
        return total[:, :frames] + total[:, frames:]

    basis = lax.fori_loop(0, ITERS, lambda _, rows: orthonormal_rows(update(project(rows))), basis)
    return basis, project(basis)


def shrunk(value, level):
    return value - jnp.clip(value, -level, level)


def inner_rows(tiles, patch, place):
    lane = lane_ids((GROUP, LANES))
    for p in range(1, 9):
        if patch == 0:
            tile, turn = (4, -MARGIN) if p == 8 else (p % 4, -MARGIN - HALF * (p // 4))
            shared, at = (5, SHARED * p) if 4 <= p < 8 else (4, HALF + SHARED * (p % 8))
            from_own = lane < HALF - MARGIN
        else:
            tile, turn = (5, HALF + MARGIN) if p == 8 else (p % 4, HALF + MARGIN - HALF * (p // 4))
            shared, at = 4, SHARED * (p % 8)
            from_own = lane >= HALF + MARGIN
        own = pltpu.roll(tiles[tile], turn % LANES, 1)
        both = pltpu.roll(tiles[shared], (HALF - MARGIN - at) % LANES, 1)
        place(p, jnp.where(from_own, own, both))


def finish(patch, odd, basis, level, means, projected, packed, outs, earlier):
    spatial_ref, mean_ref, basis_ref = outs
    tiles = 6
    rows = tiles * GROUP
    keep = lane_ids((GROUP, LANES)) < HALF
    spots = [
        pl.ds(pl.multiple_of(GROUP * jnp.where(odd == 0, p - 1, 8 - p), GROUP), GROUP)
        for p in range(9)
    ]

    def place_mean(p, value):
        if patch == 1:
            value = jnp.where(keep, earlier[1][spots[p], :], value)
        mean_ref[spots[p], :] = value

    inner_rows([means[GROUP * i : GROUP * i + GROUP, :] for i in range(tiles)], patch, place_mean)
    for row in range(rows):
        packed[pl.ds(row, RANK, stride=rows), :] = shrunk(
            projected[:, row * LANES : (row + 1) * LANES], level
        )
    for part in range(RANK):
        base = part * rows

        def place(p, value):
            if patch == 1:
                value = jnp.where(keep, earlier[0][part, spots[p], :], value)
            spatial_ref[part, spots[p], :] = value

        inner_rows(
            [packed[base + GROUP * i : base + GROUP * i + GROUP, :] for i in range(tiles)],
            patch,
            place,
        )
    scaled = basis * jnp.sqrt(jnp.float32(basis.shape[1]))
    if patch == 0:
        basis_ref[...] = scaled
    else:
        basis_ref[0] = earlier[2][...]
        basis_ref[1] = scaled


SHARED_AT = SECOND_ROWS
PIXEL_ROWS = EDGE * EDGE // LANES


def patch_0_kernel(
    odd_ref, first_ref, edge_ref, far_ref, start_ref, *refs
):
    spatial_ref, mean_ref, basis_ref, next_movie, next_means = refs[:5]
    raw, movie, means, projected, packed, sems = refs[5:]
    frames = first_ref.shape[0]
    sources = [(first_ref, g) for g in (2, 3, 4, 5, 0, 1)] + [(edge_ref, 0), (edge_ref, 1)]
    copies = [tile_copy(ref, g, raw.at[i], sems.at[i]) for i, (ref, g) in enumerate(sources)]
    for copy in copies:
        copy.start()

    def read(i, s):
        return raw[i, pl.ds(s, frames, stride=GROUP), :]

    for i in range(5):
        copies[i].wait()

        @pl.loop(0, GROUP)
        def _(s, i=i):
            keep_row(GROUP * i + s, read(i, s), movie, means)

    for copy in copies[5:]:
        copy.wait()
    lower = lane_ids((frames, LANES)) < HALF

    @pl.loop(0, GROUP)
    def _(s):
        edge = read(5, s)
        keep_row(40 + s, jnp.where(lower, read(6, s), edge), movie, means)
        both = jnp.where(lower, pltpu.roll(read(4, s), HALF, 1), edge)
        keep_row(s, both, next_movie, next_means)
        both = jnp.where(lower, edge, pltpu.roll(read(7, s), HALF, 1))
        keep_row(GROUP + s, both, next_movie, next_means)

    near = narrow_rows(raw.at[6], HALF)
    far = far_ref[...]
    keep_row(48, near, movie, means)
    keep_row(49, far, movie, means)
    keep_row(16, near, next_movie, next_means)
    keep_row(17, far, next_movie, next_means)
    width = 5 * 2 * LANES
    chunks = [(movie, k, width, k) for k in range(0, PIXEL_ROWS * LANES, width)]
    basis, level = iterate(start_ref[...], chunks, projected, frames)
    outs = (spatial_ref, mean_ref, basis_ref)
    finish(0, odd_ref[0], basis, level, means, projected, packed, outs, None)


def patch_1_kernel(odd_ref, second_ref, next_movie, next_means, start_ref, *refs):
    earlier, outs = refs[:3], refs[3:6]
    movie, means, projected, packed = refs[6:]
    rows = SECOND_ROWS
    frames = second_ref.shape[0] // rows

    @pl.loop(0, rows)
    def _(row):
        keep_row(row, second_ref[pl.ds(row, frames, stride=rows), :], movie, means)

    means[rows : rows + 2 * GROUP, :] = next_means[0 : 2 * GROUP, :]
    own = rows * LANES
    chunks = [(movie, k, 1024, k) for k in range(0, own, 1024)]
    chunks += [(next_movie, k, 1152, own + k) for k in (0, 1152)]
    basis, level = iterate(start_ref[...], chunks, projected, frames)
    finish(1, odd_ref[0], basis, level, means, projected, packed, outs, earlier)


def decompose(patch, *operands):
    frames = operands[1].shape[0]
    smem = pl.BlockSpec(memory_space=pltpu.SMEM)
    vmem = pl.BlockSpec(memory_space=pltpu.VMEM)
    hbm = pl.BlockSpec(memory_space=pltpu.HBM)
    bases = (RANK, frames) if patch == 0 else (2, RANK, frames)
    shapes = [
        jax.ShapeDtypeStruct((RANK, PATCH, LANES), jnp.float32),
        jax.ShapeDtypeStruct((PATCH, LANES), jnp.float32),
        jax.ShapeDtypeStruct(bases, jnp.float32),
    ]
    later = PIXEL_ROWS - SECOND_ROWS
    scratch = [
        pltpu.VMEM((2 * frames, (PIXEL_ROWS - later * patch) * LANES), jnp.bfloat16),
        pltpu.VMEM((56, LANES), jnp.float32),
        pltpu.VMEM((RANK, PIXEL_ROWS * LANES), jnp.float32),
        pltpu.VMEM((RANK * 48, LANES), jnp.float32),
    ]
    if patch == 0:
        in_specs = [smem, hbm, hbm, vmem, vmem]
        shapes += [
            jax.ShapeDtypeStruct((2 * frames, later * LANES), jnp.bfloat16),
            jax.ShapeDtypeStruct((24, LANES), jnp.float32),
        ]
        scratch = [pltpu.VMEM((8, frames * GROUP, LANES), jnp.float32), *scratch]
        scratch.append(pltpu.SemaphoreType.DMA((8,)))
    else:
        operands = (
            operands[0], operands[1].reshape(frames * SECOND_ROWS, LANES), *operands[2:]
        )
        in_specs = [smem] + [vmem] * 7
    return pl.pallas_call(
        patch_1_kernel if patch else patch_0_kernel,
        out_shape=tuple(shapes),
        in_specs=in_specs,
        out_specs=(vmem,) * len(shapes),
        scratch_shapes=scratch,
        compiler_params=pltpu.CompilerParams(vmem_limit_bytes=32 << 20),
        cost_estimate=pl.CostEstimate(
            flops=26 * 64 * 256 * PIXEL_ROWS * LANES,
            bytes_accessed=4 * frames * PIXEL_ROWS * LANES,
            transcendentals=0,
        ),
        name="patch_1" if patch else "patch_0",
    )(*operands)


def on_device(frames, shifts, start_basis):
    n_rows = lax.axis_size("py")
    n_cols = lax.axis_size("px")
    odd = (lax.axis_index("py") % 2).astype(jnp.int32).reshape(1)
    first, second = spread(frames[0], shifts, n_rows, n_cols)
    first = lax.all_to_all(first, ("px", "py"), split_axis=0, concat_axis=0, tiled=True)
    second = lax.all_to_all(second, ("px", "py"), split_axis=0, concat_axis=0, tiled=True)
    start = start_rows(start_basis.T)
    edge, far = pack(first)
    pairs = [(i, i ^ 1) for i in range(n_rows)]
    edge = lax.ppermute(edge, "py", pairs)
    across = [(i, i + 1 if i % 2 else i - 1) for i in range(1, n_rows - 1)]
    far = lax.ppermute(far, "py", across)
    *left, next_movie, next_means = decompose(0, odd, first, edge, far, start)
    spatial, background, bases = decompose(
        1, odd, second, next_movie, next_means, start, *left
    )
    return (spatial, bases.swapaxes(1, 2)[None], background)


def solution(mesh):
    placed = (P(("px", "py"), None, None), P(("px", "py"), None), P())
    return jax.shard_map(
        on_device,
        mesh=mesh,
        in_specs=placed,
        out_specs=(P(None, "py", "px"), P("py", "px", None, None), P("py", "px")),
        check_vma=False,
    )
```

time: 137 us -> 157 us (1.15)
  Pallas kernels: 55.2 us -> 83.5 us
  waiting for transfers between devices: 9.23 us -> 0.8 us
  starting transfers between devices: 5.48 us -> 11.8 us
  blocking collectives: 58.2 us -> 52.3 us
    pallas_call x2 -> x3, Pallas kernels: 42.5 us -> 75.1 us  [the longest x2 41.6 us: decompose(): pl.pallas_call(patch_1_kernel if patch else patch_0_kernel, out_shape=tup...]
    all_to_all x1, waiting for transfers between devices: 9.23 us -> 0.01 us  [on_device(): lax.all_to_all(second, ('px', 'py'), split_axis=0, concat_axis=0, tiled=T...]
    all_to_all x1, blocking collectives: 58.2 us -> 52.3 us  [on_device(): lax.all_to_all(first, ('px', 'py'), split_axis=0, concat_axis=0, tiled=True)]
    ppermute x0 -> x2, starting transfers between devices: none -> 5.79 us  [the longest x1 4.43 us: on_device(): far = lax.ppermute(far, 'py', across)]
    pallas_call x1, Pallas kernels: 10.6 us -> 6.36 us  [spread(): pl.pallas_call(spread_kernel, grid=(n_rows,), out_shape=(shape(FIRST_ROWS...]
    unnamed x15 -> x20, local copies, waits for them, and re-layouts: 8.29 us -> 7.68 us
  transfers between devices with their start and end apart: 1 -> 3, of which waited for: 1 -> 1; matrix products, arithmetic and copies ran while one was open for 0% -> 0% of each run, Pallas kernels for 17% -> 35%
where the time goes in v1:
time: 157 us
  Pallas kernels  83.5 us (53%)
  blocking collectives  52.3 us (33%)
  starting transfers between devices  11.8 us (8%)
  local copies, waits for them, and re-layouts  7.68 us (5%)
    all_to_all x1, blocking collectives, on_device(): lax.all_to_all(first, ('px', 'py'), split_axis=0, concat_axis=0, tiled=True)  52.3 us
    pallas_call x2, Pallas kernels, decompose(): pl.pallas_call(patch_1_kernel if patch else patch_0_kernel, out_shape=tup...  41.6 us
    pallas_call x1, Pallas kernels, pack(): pl.pallas_call(pack_kernel, out_shape=(jax.ShapeDtypeStruct((frames, 2 *...  33.5 us
    unnamed x20, local copies, waits for them, and re-layouts  7.68 us
    pallas_call x1, Pallas kernels, spread(): pl.pallas_call(spread_kernel, grid=(n_rows,), out_shape=(shape(FIRST_ROWS...  6.36 us
    all_to_all x1, starting transfers between devices, on_device(): lax.all_to_all(second, ('px', 'py'), split_axis=0, concat_axis=0, tiled=T...  5.98 us
    ppermute x1, starting transfers between devices, on_device(): far = lax.ppermute(far, 'py', across)  4.43 us
  transfers between devices with their start and end apart: 3, of which 1 were waited for; matrix products, arithmetic and copies ran while one was open for 0% of the time, Pallas kernels for 35%

profile of v1, /device:TPU:1, one launch (start us, length us, event | category | flops | bytes accessed | tf_op | source)
XLA Modules:
  0.0 156.8 jit_solution(3756150781042846429)
XLA Ops:
  0.6 0.0 copy-start.1
  0.6 2.2 %copy-done.1 = f32[1,1024,1024]{2,1,0:T(8,128)S(1)} copy-done((f32[1,1024,1024]{2,1,0:T(8,128)S(1)}, f32[1,1024,1024]{2,1,0:T(8,128)}, u32[]{:S(2)}) %copy-start.1) | copy-done | bytes 4194328
  2.8 0.7 copy-done.5
  3.5 6.4 %spread.1 = (f32[8,16,48,128]{3,2,1,0:T(8,128)S(1)}, f32[8,16,32,128]{3,2,1,0:T(8,128)S(1)}) custom-call(s32[1,2]{1,0:T(1,128)S(1)} %copy-done.5, f32[1024,1024]{1,0:T(8,128)S(1)} %bitcast.9), custom_call_target="tpu_custom_call" | custom-call | tf_op jit(solution)/shard_map/spread/pallas_call | solution.py:126
  9.8 0.0 copy-start.2
  9.9 52.3 %all_to_all.10.first_ref = f32[128,48,128]{2,1,0:T(8,128)} all-to-all(f32[128,48,128]{2,1,0:T(8,128)S(1)} %bitcast.10), channel_id=1, replica_groups=mesh['py'=16,'px'=8] {'px','py'}, dimensions={0} | all-to-all | bytes 6291456 | tf_op jit(solution)/shard_map/all_to_all | solution.py:502
  62.2 0.0 copy-done.2
  62.2 6.0 %all-to-all-start = ((f32[128,32,128]{2,1,0:T(8,128)}), f32[128,32,128]{2,1,0:T(8,128)}, u32[]{:S(2)}, u32[]{:S(2)}) async-start(f32[128,32,128]{2,1,0:T(8,128)} %bitcast.11), calls=%async_computation | async-start | bytes 4194304 | tf_op jit(solution)/shard_map/all_to_all | solution.py:503
  68.2 33.5 %pack.1 = (f32[128,16,128]{2,1,0:T(8,128)}, f32[128,128]{1,0:T(8,128)}) custom-call(f32[128,48,128]{2,1,0:T(8,128)} %all_to_all.10.first_ref), custom_call_target="tpu_custom_call" | custom-call | tf_op jit(solution)/shard_map/pack/pallas_call | solution.py:181
  101.7 1.4 collective-permute-start
  103.1 4.4 %collective-permute-start.1 = (f32[128,128]{1,0:T(8,128)}, f32[128,128]{1,0:T(8,128)S(1)}, u32[]{:S(2)}, u32[]{:S(2)}) collective-permute-start(f32[128,128]{1,0:T(8,128)} %get-tuple-element.18), channel_id=1, source_target_pairs={{8,16},{16,8},{24,32},{32,24},{40,48},{48,40},{56,64},{64,56},{72,... | collective-permute-start | bytes 196616 | tf_op jit(solution)/shard_map/ppermute | solution.py:509
  107.5 2.0 %start_rows.1.start_ref = f32[16,128]{1,0:T(8,128)} custom-call(f32[16,128]{1,0:T(8,128)} %bitcast.12), custom_call_target="tpu_custom_call" | custom-call | tf_op jit(solution)/shard_map/start_rows/pallas_call | solution.py:259
  109.6 0.8 collective-permute-done.1.far_ref
  110.4 0.0 collective-permute-done.edge_ref
  110.4 0.0 copy-done
  110.4 0.7 copy-done.3
  111.1 19.8 %patch_0.1 = (f32[16,64,128]{2,1,0:T(8,128)S(1)}, f32[64,128]{1,0:T(8,128)S(1)}, f32[16,128]{1,0:T(8,128)S(1)}, bf16[256,2304]{1,0:T(8,128)(2,1)S(1)}, f32[24,128]{1,0:T(8,128)S(1)}) custom-call(s32[1]{0:T(128)} %bitcast.odd_ref, f32[128,48,128]{2,1,0:T(8,128)S(1)} %copy-done, f32[128,16,128]{2,1,0:T(8,128)} %collective-permute-done.edge_ref, ...), custom_call_target="tpu_custom_call" | custom-call | flops 2726297600 | bytes 3276800 | tf_op jit(solution)/shard_map/patch_0/pallas_call | solution.py:481
  130.9 0.0 copy-start.6
  130.9 1.0 copy-done.6
  132.0 0.8 copy-done.8
  132.7 0.0 all-to-all-done
  132.8 1.3 copy-done.7
  134.0 1.0 copy-done.9
  135.1 21.8 %patch_1.1 = (f32[16,64,128]{2,1,0:T(8,128)}, f32[64,128]{1,0:T(8,128)}, f32[2,16,128]{2,1,0:T(8,128)}) custom-call(s32[1]{0:T(128)} %bitcast.odd_ref, f32[4096,128]{1,0:T(8,128)} %bitcast.3.second_ref, bf16[256,2304]{1,0:T(8,128)(2,1)S(1)} %copy-done.7, f32[24,128]{1,0:T(8,128)S(1)} %get-tuple-element.20.next_means, f32[16,128]{1,0:T(8,128)S(1)} %copy-done.4, ...), custom_call_target="tpu_custom_call" | custom-call | flops 2726297600 | bytes 3276800 | tf_op jit(solution)/shard_map/patch_1/pallas_call | solution.py:481
  (8 shorter events, 0.0 us)
Async XLA Ops:
  0.6 2.2 %copy-start.1 = (f32[1,1024,1024]{2,1,0:T(8,128)S(1)}, f32[1,1024,1024]{2,1,0:T(8,128)}, u32[]{:S(2)}) copy-start(f32[1,1024,1024]{2,1,0:T(8,128)} %param.3) | copy-start | bytes 12582916
  2.8 0.7 copy-start.5
  9.8 52.3 %copy-start.2 = (f32[8,16,32,128]{3,2,1,0:T(8,128)}, f32[8,16,32,128]{3,2,1,0:T(8,128)S(1)}, u32[]{:S(2)}) copy-start(f32[8,16,32,128]{3,2,1,0:T(8,128)S(1)} %get-tuple-element.15) | copy-start | bytes 6291460
  62.2 48.2 %copy-start = (f32[128,48,128]{2,1,0:T(8,128)S(1)}, f32[128,48,128]{2,1,0:T(8,128)}, u32[]{:S(2)}) copy-start(f32[128,48,128]{2,1,0:T(8,128)} %all_to_all.10.first_ref) | copy-start | bytes 9437188
  62.2 70.5 %all-to-all-start = ((f32[128,32,128]{2,1,0:T(8,128)}), f32[128,32,128]{2,1,0:T(8,128)}, u32[]{:S(2)}, u32[]{:S(2)}) async-start(f32[128,32,128]{2,1,0:T(8,128)} %bitcast.11), calls=%async_computation | async-start | bytes 4194304 | tf_op jit(solution)/shard_map/all_to_all | solution.py:503
  101.7 8.7 %collective-permute-start = (f32[128,16,128]{2,1,0:T(8,128)}, f32[128,16,128]{2,1,0:T(8,128)}, u32[]{:S(2)}, u32[]{:S(2)}) collective-permute-start(f32[128,16,128]{2,1,0:T(8,128)} %get-tuple-element.17), channel_id=1, source_target_pairs={{0,8},{8,0},{16,24},{24,16},{32,40},{40,32},{48,56},{56,48},{64,72... | collective-permute-start | bytes 3145736 | tf_op jit(solution)/shard_map/ppermute | solution.py:507
  103.1 7.3 %collective-permute-start.1 = (f32[128,128]{1,0:T(8,128)}, f32[128,128]{1,0:T(8,128)S(1)}, u32[]{:S(2)}, u32[]{:S(2)}) collective-permute-start(f32[128,128]{1,0:T(8,128)} %get-tuple-element.18), channel_id=1, source_target_pairs={{8,16},{16,8},{24,32},{32,24},{40,48},{48,40},{56,64},{64,56},{72,... | collective-permute-start | bytes 196616 | tf_op jit(solution)/shard_map/ppermute | solution.py:509
  110.4 0.7 copy-start.3
  111.1 21.7 %copy-start.4 = (f32[16,128]{1,0:T(8,128)S(1)}, f32[16,128]{1,0:T(8,128)}, u32[]{:S(2)}) copy-start(f32[16,128]{1,0:T(8,128)} %start_rows.1.start_ref) | copy-start | bytes 24580
  130.9 1.0 copy-start.6
  131.9 0.8 copy-start.8
  132.7 1.3 copy-start.7
  134.0 1.0 copy-start.9

commit v2 on v1

--- a/solution.py
+++ b/solution.py
@@ -19,8 +19,8 @@
 HALF = 64
 SHARED = 16
 FIRST_ROWS = 48
+UNROLL = 4
 SECOND_ROWS = 32
-HIGH = lax.Precision.HIGHEST
 
 
 def lane_ids(shape):
@@ -135,7 +135,7 @@
             pltpu.SemaphoreType.DMA((height // PATCH,)),
             pltpu.SemaphoreType.DMA,
         ],
-        compiler_params=pltpu.CompilerParams(vmem_limit_bytes=24 << 20),
+        compiler_params=pltpu.CompilerParams(vmem_limit_bytes=60 << 20),
         name="spread",
     )(shifts, frame)
     peers = n_rows * n_cols
@@ -185,14 +185,12 @@
             jax.ShapeDtypeStruct((frames, LANES), jnp.float32),
         ),
         in_specs=[pl.BlockSpec(memory_space=pltpu.HBM)],
-        out_specs=(
-            pl.BlockSpec(memory_space=pltpu.HBM),
-            pl.BlockSpec(memory_space=pltpu.VMEM),
-        ),
+        out_specs=(pl.BlockSpec(memory_space=pltpu.VMEM),) * 2,
         scratch_shapes=[
             pltpu.VMEM((frames * GROUP, LANES), jnp.float32),
             pltpu.SemaphoreType.DMA((2,)),
         ],
+        compiler_params=pltpu.CompilerParams(vmem_limit_bytes=60 << 20),
         name="pack",
     )(first)
 
@@ -203,14 +201,24 @@
     return high, low
 
 
-def eliminate(gram, rows):
+def eliminate(rows):
     count, width = rows.shape
     half = count // 2
-    column = [jnp.broadcast_to(gram[:, k : k + 1], (count, width)) for k in range(count)]
-    upper = [c[:half] for c in column]
-    lower = [c[half:] for c in column]
     row_id = lax.broadcasted_iota(jnp.int32, (half, width), 0)
     top, bottom = rows[:half], rows[half:]
+
+    def products(part, other):
+        return jnp.broadcast_to(jnp.sum(part * other, axis=1, keepdims=True), part.shape)
+
+    upper, lower = [], []
+    for k in range(count):
+        at = k % half
+        ridge = jnp.where(row_id == at, EPSILON, 0.0)
+        if k < half:
+            upper.append(products(top, top[at : at + 1]) + ridge)
+            lower.append(products(bottom, top[at : at + 1]))
+        else:
+            lower.append(products(bottom, bottom[at : at + 1]) + ridge)
     for j in range(count):
         at = j % half
         source = upper[j] if j < half else lower[j]
@@ -240,15 +248,7 @@
 
 
 def orthonormal_rows(rows):
-    count = rows.shape[0]
-    across = lax.broadcasted_iota(jnp.int32, (count, count), 0)
-    ident = jnp.where(across == lane_ids((count, count)), EPSILON, 0.0)
-    for sweep in range(2):
-        gram = lax.dot_general(
-            rows, rows, (((1,), (1,)), ((), ())), precision=HIGH, preferred_element_type=jnp.float32
-        )
-        rows = eliminate(gram + ident, rows)
-    return rows
+    return lax.fori_loop(0, 2, lambda _, z: eliminate(z), rows)
 
 
 def orth_kernel(start_ref, out_ref):
@@ -261,6 +261,7 @@
         out_shape=jax.ShapeDtypeStruct(start.shape, jnp.float32),
         in_specs=[pl.BlockSpec(memory_space=pltpu.VMEM)],
         out_specs=pl.BlockSpec(memory_space=pltpu.VMEM),
+        compiler_params=pltpu.CompilerParams(vmem_limit_bytes=60 << 20),
         name="start_rows",
     )(start)
 
@@ -271,49 +272,46 @@
     return mean, split(values - mean)
 
 
-def keep_row(row, values, movie, means):
+def keep_row(row, values, movie, turned, means):
     frames = values.shape[0]
     mean, (high, low) = centred(values)
     means[pl.ds(row, 1), :] = mean
-    lanes = pl.ds(pl.multiple_of(row * LANES, LANES), LANES)
-    movie[0:frames, lanes] = high
-    movie[frames:, lanes] = low
-
-
-def iterate(basis, chunks, projected, frames):
+    pixels = pl.ds(pl.multiple_of(row * LANES, LANES), LANES)
+    movie[0:frames, pixels] = high
+    movie[frames:, pixels] = low
+    turned[pixels, 0:frames] = high.T
+    turned[pixels, frames:] = low.T
+
+
+def iterate(basis, movie, turned, projected, frames, once):
     def project(basis):
         high, low = split(basis)
         left = jnp.concatenate(
             [jnp.concatenate([high, high], axis=1), jnp.concatenate([low, low], axis=1)], axis=0
         )
+        both = jnp.dot(left, movie[...], preferred_element_type=jnp.float32)
+        value = both[:RANK] + both[RANK:]
+        projected[...] = value
         total = jnp.zeros((RANK, LANES), jnp.float32)
-        for movie, start, width, here in chunks:
-            both = jnp.dot(
-                left, movie[:, start : start + width], preferred_element_type=jnp.float32
-            )
-            value = both[:RANK] + both[RANK:]
-            projected[:, here : here + width] = value
-            for k in range(0, width, LANES):
-                piece = value[:, k : k + LANES]
-                total = total + piece * piece
+        for k in range(0, value.shape[1], LANES):
+            piece = value[:, k : k + LANES]
+            total = total + piece * piece
         mean_square = jnp.sum(total, axis=1, keepdims=True) * (1.0 / (EDGE * EDGE))
         return SHRINK * jnp.sqrt(mean_square + EPSILON)
 
     def update(level):
-        total = jnp.zeros((2 * RANK, 2 * frames), jnp.float32)
-        for movie, start, width, here in chunks:
-            factor = shrunk(projected[:, here : here + width], level)
-            left = jnp.concatenate(split(factor), axis=0)
-            total = total + lax.dot_general(
-                left,
-                movie[:, start : start + width],
-                (((1,), (1,)), ((), ())),
-                preferred_element_type=jnp.float32,
-            )
+        factor = shrunk(projected[...], level)
+        left = jnp.concatenate(split(factor), axis=0)
+        total = jnp.dot(left, turned[...], preferred_element_type=jnp.float32)
         total = total[:RANK] + total[RANK:]
         return total[:, :frames] + total[:, frames:]
 
-    basis = lax.fori_loop(0, ITERS, lambda _, rows: orthonormal_rows(update(project(rows))), basis)
+    def step(_, rows):
+        level = jnp.zeros((RANK, 1), jnp.float32)
+        level = lax.fori_loop(0, once, lambda _, level: project(rows), level)
+        return orthonormal_rows(update(level))
+
+    basis = lax.fori_loop(0, ITERS, step, basis)
     return basis, project(basis)
 
 
@@ -360,7 +358,7 @@
     for part in range(RANK):
         base = part * rows
 
-        def place(p, value):
+        def place(p, value, part=part):
             if patch == 1:
                 value = jnp.where(keep, earlier[0][part, spots[p], :], value)
             spatial_ref[part, spots[p], :] = value
@@ -378,20 +376,25 @@
         basis_ref[1] = scaled
 
 
-SHARED_AT = SECOND_ROWS
 PIXEL_ROWS = EDGE * EDGE // LANES
-
-
-def patch_0_kernel(
-    odd_ref, first_ref, edge_ref, far_ref, start_ref, *refs
-):
-    spatial_ref, mean_ref, basis_ref, next_movie, next_means = refs[:5]
-    raw, movie, means, projected, packed, sems = refs[5:]
+NEXT_ROWS = PIXEL_ROWS - SECOND_ROWS
+
+
+def patch_0_kernel(odd_ref, first_ref, edge_ref, far_ref, start_ref, *refs):
+    spatial_ref, mean_ref, basis_ref, next_means, next_movie_out, next_turned_out = refs[:6]
+    raw, far, start, movie, turned, next_movie, next_turned = refs[6:13]
+    means, projected, packed, sems = refs[13:]
     frames = first_ref.shape[0]
     sources = [(first_ref, g) for g in (2, 3, 4, 5, 0, 1)] + [(edge_ref, 0), (edge_ref, 1)]
     copies = [tile_copy(ref, g, raw.at[i], sems.at[i]) for i, (ref, g) in enumerate(sources)]
+    copies.append(pltpu.make_async_copy(far_ref, far, sems.at[8]))
+    copies.append(pltpu.make_async_copy(start_ref, start, sems.at[9]))
     for copy in copies:
         copy.start()
+    results = [
+        pltpu.make_async_copy(next_movie, next_movie_out, sems.at[10]),
+        pltpu.make_async_copy(next_turned, next_turned_out, sems.at[11]),
+    ]
 
     def read(i, s):
         return raw[i, pl.ds(s, frames, stride=GROUP), :]
@@ -399,92 +402,123 @@
     for i in range(5):
         copies[i].wait()
 
-        @pl.loop(0, GROUP)
+        @pl.loop(0, GROUP, unroll=UNROLL)
         def _(s, i=i):
-            keep_row(GROUP * i + s, read(i, s), movie, means)
+            keep_row(GROUP * i + s, read(i, s), movie, turned, means)
 
     for copy in copies[5:]:
         copy.wait()
     lower = lane_ids((frames, LANES)) < HALF
 
-    @pl.loop(0, GROUP)
+    @pl.loop(0, GROUP, unroll=2)
     def _(s):
         edge = read(5, s)
-        keep_row(40 + s, jnp.where(lower, read(6, s), edge), movie, means)
+        keep_row(40 + s, jnp.where(lower, read(6, s), edge), movie, turned, means)
         both = jnp.where(lower, pltpu.roll(read(4, s), HALF, 1), edge)
-        keep_row(s, both, next_movie, next_means)
+        keep_row(s, both, next_movie, next_turned, next_means)
         both = jnp.where(lower, edge, pltpu.roll(read(7, s), HALF, 1))
-        keep_row(GROUP + s, both, next_movie, next_means)
-
+        keep_row(GROUP + s, both, next_movie, next_turned, next_means)
+
+    once = (odd_ref[0] >= 0).astype(jnp.int32)
     near = narrow_rows(raw.at[6], HALF)
-    far = far_ref[...]
-    keep_row(48, near, movie, means)
-    keep_row(49, far, movie, means)
-    keep_row(16, near, next_movie, next_means)
-    keep_row(17, far, next_movie, next_means)
-    width = 5 * 2 * LANES
-    chunks = [(movie, k, width, k) for k in range(0, PIXEL_ROWS * LANES, width)]
-    basis, level = iterate(start_ref[...], chunks, projected, frames)
+    for row, values in ((0, near), (1, far[...])):
+        keep_row(48 + row, values, movie, turned, means)
+        keep_row(2 * GROUP + row, values, next_movie, next_turned, next_means)
+    for copy in results:
+        copy.start()
+    basis, level = iterate(start[...], movie, turned, projected, frames, once)
     outs = (spatial_ref, mean_ref, basis_ref)
     finish(0, odd_ref[0], basis, level, means, projected, packed, outs, None)
-
-
-def patch_1_kernel(odd_ref, second_ref, next_movie, next_means, start_ref, *refs):
-    earlier, outs = refs[:3], refs[3:6]
-    movie, means, projected, packed = refs[6:]
-    rows = SECOND_ROWS
-    frames = second_ref.shape[0] // rows
-
-    @pl.loop(0, rows)
-    def _(row):
-        keep_row(row, second_ref[pl.ds(row, frames, stride=rows), :], movie, means)
-
-    means[rows : rows + 2 * GROUP, :] = next_means[0 : 2 * GROUP, :]
-    own = rows * LANES
-    chunks = [(movie, k, 1024, k) for k in range(0, own, 1024)]
-    chunks += [(next_movie, k, 1152, own + k) for k in (0, 1152)]
-    basis, level = iterate(start_ref[...], chunks, projected, frames)
+    for copy in results:
+        copy.wait()
+
+
+def patch_1_kernel(
+    odd_ref, second_ref, next_movie_in, next_turned_in, next_means_in, start_ref, *refs
+):
+    earlier_in, outs = refs[:3], refs[3:6]
+    raw, start, next_means = refs[6:9]
+    earlier = refs[9:12]
+    movie, turned, means, projected, packed, sems = refs[12:]
+    own = SECOND_ROWS * LANES
+    frames = second_ref.shape[0]
+    tiles = SECOND_ROWS // GROUP
+    copies = [tile_copy(second_ref, i, raw.at[i], sems.at[i]) for i in range(tiles)]
+    sources = (next_movie_in, next_turned_in, next_means_in, start_ref, *earlier_in)
+    targets = (movie.at[:, own:], turned.at[own:, :], next_means, start, *earlier)
+    for i, (source, target) in enumerate(zip(sources, targets)):
+        copies.append(pltpu.make_async_copy(source, target, sems.at[tiles + i]))
+    for copy in copies:
+        copy.start()
+    for i in range(tiles):
+        copies[i].wait()
+
+        @pl.loop(0, GROUP, unroll=UNROLL)
+        def _(s, i=i):
+            values = raw[i, pl.ds(s, frames, stride=GROUP), :]
+            keep_row(GROUP * i + s, values, movie, turned, means)
+
+    for copy in copies[tiles:]:
+        copy.wait()
+    once = (odd_ref[0] >= 0).astype(jnp.int32)
+    means[SECOND_ROWS : SECOND_ROWS + 2 * GROUP, :] = next_means[0 : 2 * GROUP, :]
+    basis, level = iterate(start[...], movie, turned, projected, frames, once)
     finish(1, odd_ref[0], basis, level, means, projected, packed, outs, earlier)
 
 
 def decompose(patch, *operands):
     frames = operands[1].shape[0]
-    smem = pl.BlockSpec(memory_space=pltpu.SMEM)
     vmem = pl.BlockSpec(memory_space=pltpu.VMEM)
     hbm = pl.BlockSpec(memory_space=pltpu.HBM)
+    def parts(rows, make):
+        return [
+            make((2 * frames, rows * LANES), jnp.bfloat16),
+            make((rows * LANES, 2 * frames), jnp.bfloat16),
+        ]
+
     bases = (RANK, frames) if patch == 0 else (2, RANK, frames)
     shapes = [
         jax.ShapeDtypeStruct((RANK, PATCH, LANES), jnp.float32),
         jax.ShapeDtypeStruct((PATCH, LANES), jnp.float32),
         jax.ShapeDtypeStruct(bases, jnp.float32),
     ]
-    later = PIXEL_ROWS - SECOND_ROWS
-    scratch = [
-        pltpu.VMEM((2 * frames, (PIXEL_ROWS - later * patch) * LANES), jnp.bfloat16),
+    out_specs = [vmem] * 3
+    start = pltpu.VMEM((RANK, frames), jnp.float32)
+    next_means = (24, LANES)
+    if patch == 0:
+        shapes.append(jax.ShapeDtypeStruct(next_means, jnp.float32))
+        shapes += parts(NEXT_ROWS, jax.ShapeDtypeStruct)
+        out_specs += [vmem, hbm, hbm]
+        scratch = [
+            pltpu.VMEM((8, frames * GROUP, LANES), jnp.float32),
+            pltpu.VMEM((frames, LANES), jnp.float32),
+            start,
+            *parts(PIXEL_ROWS, pltpu.VMEM),
+            *parts(NEXT_ROWS, pltpu.VMEM),
+        ]
+    else:
+        scratch = [
+            pltpu.VMEM((SECOND_ROWS // GROUP, frames * GROUP, LANES), jnp.float32),
+            start,
+            pltpu.VMEM(next_means, jnp.float32),
+            pltpu.VMEM(operands[6].shape, jnp.float32),
+            pltpu.VMEM(operands[7].shape, jnp.float32),
+            pltpu.VMEM(operands[8].shape, jnp.float32),
+            *parts(PIXEL_ROWS, pltpu.VMEM),
+        ]
+    scratch += [
         pltpu.VMEM((56, LANES), jnp.float32),
         pltpu.VMEM((RANK, PIXEL_ROWS * LANES), jnp.float32),
         pltpu.VMEM((RANK * 48, LANES), jnp.float32),
+        pltpu.SemaphoreType.DMA((12,)),
     ]
-    if patch == 0:
-        in_specs = [smem, hbm, hbm, vmem, vmem]
-        shapes += [
-            jax.ShapeDtypeStruct((2 * frames, later * LANES), jnp.bfloat16),
-            jax.ShapeDtypeStruct((24, LANES), jnp.float32),
-        ]
-        scratch = [pltpu.VMEM((8, frames * GROUP, LANES), jnp.float32), *scratch]
-        scratch.append(pltpu.SemaphoreType.DMA((8,)))
-    else:
-        operands = (
-            operands[0], operands[1].reshape(frames * SECOND_ROWS, LANES), *operands[2:]
-        )
-        in_specs = [smem] + [vmem] * 7
     return pl.pallas_call(
         patch_1_kernel if patch else patch_0_kernel,
         out_shape=tuple(shapes),
-        in_specs=in_specs,
-        out_specs=(vmem,) * len(shapes),
+        in_specs=[pl.BlockSpec(memory_space=pltpu.SMEM)] + [hbm] * (len(operands) - 1),
+        out_specs=tuple(out_specs),
         scratch_shapes=scratch,
-        compiler_params=pltpu.CompilerParams(vmem_limit_bytes=32 << 20),
+        compiler_params=pltpu.CompilerParams(vmem_limit_bytes=60 << 20),
         cost_estimate=pl.CostEstimate(
             flops=26 * 64 * 256 * PIXEL_ROWS * LANES,
             bytes_accessed=4 * frames * PIXEL_ROWS * LANES,
@@ -497,19 +531,19 @@
 def on_device(frames, shifts, start_basis):
     n_rows = lax.axis_size("py")
     n_cols = lax.axis_size("px")
-    odd = (lax.axis_index("py") % 2).astype(jnp.int32).reshape(1)
+    odd = (lax.axis_index("py") & 1).astype(jnp.int32).reshape(1)
     first, second = spread(frames[0], shifts, n_rows, n_cols)
     first = lax.all_to_all(first, ("px", "py"), split_axis=0, concat_axis=0, tiled=True)
-    second = lax.all_to_all(second, ("px", "py"), split_axis=0, concat_axis=0, tiled=True)
-    start = start_rows(start_basis.T)
+    first, start = lax.optimization_barrier((first, start_rows(start_basis.T)))
     edge, far = pack(first)
     pairs = [(i, i ^ 1) for i in range(n_rows)]
     edge = lax.ppermute(edge, "py", pairs)
     across = [(i, i + 1 if i % 2 else i - 1) for i in range(1, n_rows - 1)]
     far = lax.ppermute(far, "py", across)
-    *left, next_movie, next_means = decompose(0, odd, first, edge, far, start)
+    second = lax.all_to_all(second, ("px", "py"), split_axis=0, concat_axis=0, tiled=True)
+    *left, next_means, next_movie, next_turned = decompose(0, odd, first, edge, far, start)
     spatial, background, bases = decompose(
-        1, odd, second, next_movie, next_means, start, *left
+        1, odd, second, next_movie, next_turned, next_means, start, *left
     )
     return (spatial, bases.swapaxes(1, 2)[None], background)
 

time: 157 us -> 133 us (0.85); the launches traced: 157 us -> 131 us
  Pallas kernels: 83.5 us -> 48.8 us
  waiting for transfers between devices: 0.8 us -> 15 us
  local copies, waits for them, and re-layouts: 7.68 us -> 2.41 us
    pallas_call x1, Pallas kernels: 33.5 us -> 2.67 us  [pack(): pl.pallas_call(pack_kernel, out_shape=(jax.ShapeDtypeStruct((frames, 2 *...]
    ppermute x1, waiting for transfers between devices: 0.79 us -> 15 us  [on_device(): far = lax.ppermute(far, 'py', across)]
    pallas_call x2, Pallas kernels: 41.6 us -> 34.3 us  [decompose(): pl.pallas_call(patch_1_kernel if patch else patch_0_kernel, out_shape=tup...]
    unnamed x20 -> x6, local copies, waits for them, and re-layouts: 7.68 us -> 2.41 us
    pallas_call x1, Pallas kernels: 6.36 us -> 10.1 us  [spread(): pl.pallas_call(spread_kernel, grid=(n_rows,), out_shape=(shape(FIRST_ROWS...]
  transfers between devices with their start and end apart: 3 -> 3, of which waited for: 1 -> 1; matrix products, arithmetic and copies ran while one was open for 0% -> 0% of each run, Pallas kernels for 35% -> 17%
where the time goes in v2:
time: 133 us; the launch traced here: 131 us
  blocking collectives  52.5 us (39%)
  Pallas kernels  48.8 us (37%)
  waiting for transfers between devices  15 us (11%)
  starting transfers between devices  11.1 us (8%)
  local copies, waits for them, and re-layouts  2.41 us (2%)
    all_to_all x1, blocking collectives, on_device(): lax.all_to_all(first, ('px', 'py'), split_axis=0, concat_axis=0, tiled=True)  52.5 us
    pallas_call x2, Pallas kernels, decompose(): pl.pallas_call(patch_1_kernel if patch else patch_0_kernel, out_shape=tup...  34.3 us
    ppermute x1, waiting for transfers between devices, on_device(): far = lax.ppermute(far, 'py', across)  15 us
    pallas_call x1, Pallas kernels, spread(): pl.pallas_call(spread_kernel, grid=(n_rows,), out_shape=(shape(FIRST_ROWS...  10.1 us
    all_to_all x1, starting transfers between devices, on_device(): lax.all_to_all(second, ('px', 'py'), split_axis=0, concat_axis=0, tiled=T...  5.47 us
    ppermute x1, starting transfers between devices, on_device(): far = lax.ppermute(far, 'py', across)  4.5 us
    pallas_call x1, Pallas kernels, pack(): pl.pallas_call(pack_kernel, out_shape=(jax.ShapeDtypeStruct((frames, 2 *...  2.67 us
  transfers between devices with their start and end apart: 3, of which 1 were waited for; matrix products, arithmetic and copies ran while one was open for 0% of the time, Pallas kernels for 17%

profile of v2, /device:TPU:1, one launch (start us, length us, event | category | flops | bytes accessed | tf_op | source)
XLA Modules:
  0.0 130.7 jit_solution(12121271903004497582)
XLA Ops:
  0.6 10.1 %spread.1 = (f32[8,16,48,128]{3,2,1,0:T(8,128)}, f32[8,16,32,128]{3,2,1,0:T(8,128)}) custom-call(s32[1,2]{1,0:T(1,128)} %shifts_hbm.1, f32[1024,1024]{1,0:T(8,128)} %bitcast.8), custom_call_target="tpu_custom_call" | custom-call | tf_op jit(solution)/shard_map/spread/pallas_call | solution.py:126
  10.7 52.5 %all_to_all.10.first_ref = f32[128,48,128]{2,1,0:T(8,128)} all-to-all(f32[128,48,128]{2,1,0:T(8,128)} %bitcast.9), channel_id=1, replica_groups=mesh['py'=16,'px'=8] {'px','py'}, dimensions={0} | all-to-all | bytes 6291456 | tf_op jit(solution)/shard_map/all_to_all | solution.py:536
  63.3 5.5 %all-to-all-start = ((f32[128,32,128]{2,1,0:T(8,128)}), f32[128,32,128]{2,1,0:T(8,128)S(1)}, u32[]{:S(2)}, u32[]{:S(2)}) async-start(f32[128,32,128]{2,1,0:T(8,128)} %bitcast.10), calls=%async_computation | async-start | bytes 4194304 | tf_op jit(solution)/shard_map/all_to_all | solution.py:543
  68.8 1.8 %start_rows.1.start_ref = f32[16,128]{1,0:T(8,128)} custom-call(f32[16,128]{1,0:T(8,128)} %bitcast.11), custom_call_target="tpu_custom_call" | custom-call | tf_op jit(solution)/shard_map/start_rows/pallas_call | solution.py:259
  70.5 2.7 %pack.1 = (f32[128,16,128]{2,1,0:T(8,128)}, f32[128,128]{1,0:T(8,128)}) custom-call(f32[128,48,128]{2,1,0:T(8,128)} %all_to_all.10.first_ref), custom_call_target="tpu_custom_call" | custom-call | tf_op jit(solution)/shard_map/pack/pallas_call | solution.py:181
  73.2 1.1 collective-permute-start
  74.4 4.5 %collective-permute-start.1 = (f32[128,128]{1,0:T(8,128)}, f32[128,128]{1,0:T(8,128)S(1)}, u32[]{:S(2)}, u32[]{:S(2)}) collective-permute-start(f32[128,128]{1,0:T(8,128)} %get-tuple-element.22), channel_id=1, source_target_pairs={{8,16},{16,8},{24,32},{32,24},{40,48},{48,40},{56,64},{64,56},{72,... | collective-permute-start | bytes 196616 | tf_op jit(solution)/shard_map/ppermute | solution.py:542
  78.9 15.0 %collective-permute-done.1.far_ref = f32[128,128]{1,0:T(8,128)S(1)} collective-permute-done((f32[128,128]{1,0:T(8,128)}, f32[128,128]{1,0:T(8,128)S(1)}, u32[]{:S(2)}, u32[]{:S(2)}) %collective-permute-start.1) | collective-permute-done | bytes 65568 | tf_op jit(solution)/shard_map/ppermute | solution.py:542
  93.9 0.0 copy-start.2
  93.9 0.0 collective-permute-done.edge_ref
  93.9 0.0 copy-start.1
  93.9 0.6 copy-done.2
  94.5 0.5 copy-done.1
  95.0 18.3 %patch_0.1 = (f32[16,64,128]{2,1,0:T(8,128)}, f32[64,128]{1,0:T(8,128)}, f32[16,128]{1,0:T(8,128)}, f32[24,128]{1,0:T(8,128)}, bf16[256,2304]{1,0:T(8,128)(2,1)}, /*index=5*/bf16[2304,256]{1,0:T(8,128)(2,1)}) custom-call(s32[1]{0:T(128)} %bitcast.odd_ref, f32[128,48,128]{2,1,0:T(8,128)} %all_to_all.10.first_ref, f32[128,16,128]{2,1,0:T(8,128)} %copy-done.1, ...), custom_call_target="tpu_custom_call" | custom-call | flops 2726297600 | bytes 3276800 | tf_op jit(solution)/shard_map/patch_0/pallas_call | solution.py:515
  113.3 0.0 all-to-all-done.second_ref
  113.3 0.0 copy-start
  113.3 1.3 %copy-done = f32[128,32,128]{2,1,0:T(8,128)} copy-done((f32[128,32,128]{2,1,0:T(8,128)}, f32[128,32,128]{2,1,0:T(8,128)S(1)}, u32[]{:S(2)}) %copy-start) | copy-done | bytes 2097176
  114.6 16.0 %patch_1.1 = (f32[16,64,128]{2,1,0:T(8,128)}, f32[64,128]{1,0:T(8,128)}, f32[2,16,128]{2,1,0:T(8,128)}) custom-call(s32[1]{0:T(128)} %bitcast.odd_ref, f32[128,32,128]{2,1,0:T(8,128)} %copy-done, bf16[256,2304]{1,0:T(8,128)(2,1)} %get-tuple-element.24.next_movie_in, bf16[2304,256]{1,0:T(8,128)(2,1)} %get-tuple-element.25.next_turned_in, ...), custom_call_target="tpu_custom_call" | custom-call | flops 2726297600 | bytes 3276800 | tf_op jit(solution)/shard_map/patch_1/pallas_call | solution.py:515
Async XLA Ops:
  63.3 50.0 %all-to-all-start = ((f32[128,32,128]{2,1,0:T(8,128)}), f32[128,32,128]{2,1,0:T(8,128)S(1)}, u32[]{:S(2)}, u32[]{:S(2)}) async-start(f32[128,32,128]{2,1,0:T(8,128)} %bitcast.10), calls=%async_computation | async-start | bytes 4194304 | tf_op jit(solution)/shard_map/all_to_all | solution.py:543
  73.2 20.7 %collective-permute-start = (f32[128,16,128]{2,1,0:T(8,128)}, f32[128,16,128]{2,1,0:T(8,128)S(1)}, u32[]{:S(2)}, u32[]{:S(2)}) collective-permute-start(f32[128,16,128]{2,1,0:T(8,128)} %get-tuple-element.21), channel_id=1, source_target_pairs={{0,8},{8,0},{16,24},{24,16},{32,40},{40,32},{48,56},{56,48},{64,72... | collective-permute-start | bytes 3145736 | tf_op jit(solution)/shard_map/ppermute | solution.py:540
  74.4 19.5 %collective-permute-start.1 = (f32[128,128]{1,0:T(8,128)}, f32[128,128]{1,0:T(8,128)S(1)}, u32[]{:S(2)}, u32[]{:S(2)}) collective-permute-start(f32[128,128]{1,0:T(8,128)} %get-tuple-element.22), channel_id=1, source_target_pairs={{8,16},{16,8},{24,32},{32,24},{40,48},{48,40},{56,64},{64,56},{72,... | collective-permute-start | bytes 196616 | tf_op jit(solution)/shard_map/ppermute | solution.py:542
  93.9 0.6 copy-start.2
  93.9 1.1 copy-start.1
  113.3 1.3 %copy-start = (f32[128,32,128]{2,1,0:T(8,128)}, f32[128,32,128]{2,1,0:T(8,128)S(1)}, u32[]{:S(2)}) copy-start(f32[128,32,128]{2,1,0:T(8,128)S(1)} %all-to-all-done.second_ref) | copy-start | bytes 6291460

commit v3 on v2

--- a/solution.py
+++ b/solution.py
@@ -27,7 +27,7 @@
     return lax.broadcasted_iota(jnp.int32, shape, len(shape) - 1)
 
 
-def spread_kernel(shifts_hbm, frame_ref, first_ref, second_ref, padded, shifts_ref, sems, shift_sem):
+def spread_kernel(exchange, shifts_hbm, frame_ref, out_ref, padded, shifts_ref, sems, shift_sem):
     band = pl.program_id(0)
     height, width = frame_ref.shape
     bands = height // PATCH
@@ -100,49 +100,44 @@
         else:
             after = [jnp.where(from_here | (landing >= MARGIN), 0.0, b) for b in before]
         joined = [jnp.where(to_next, a, h) for a, h in zip(after, here)]
-        tile = rolled(here[8], 0)
-        for p in (1, 2, 3):
-            tile = jnp.where(lane >= HALF + SHARED * p, rolled(here[p], SHARED * p), tile)
-        first_ref[strip, 0, 0:8, :] = tile
-        tile = rolled(joined[8], 48)
-        for p in (4, 5, 6, 7):
-            tile = jnp.where(lane >= SHARED * p, rolled(here[p], SHARED * (p - 4)), tile)
-        first_ref[strip, 0, 8:16, :] = tile
+        if exchange == 0:
+            tile = rolled(here[8], 0)
+            for p in (1, 2, 3):
+                tile = jnp.where(lane >= HALF + SHARED * p, rolled(here[p], SHARED * p), tile)
+            out_ref[strip, 0, 0:8, :] = tile
+            tile = rolled(joined[8], 48)
+            for p in (4, 5, 6, 7):
+                tile = jnp.where(lane >= SHARED * p, rolled(here[p], SHARED * (p - 4)), tile)
+            out_ref[strip, 0, 8:16, :] = tile
+            source, amounts, base = here, (0, HALF), 2 * GROUP
+        else:
+            source, amounts, base = joined, (48, 112), 0
         for i in range(4):
-            rows = slice(GROUP * i, GROUP * i + GROUP)
-            first_ref[strip, 0, 16 + GROUP * i : 24 + GROUP * i, :] = jnp.where(
-                lower, rolled(here[i], 0), rolled(here[i + 4], HALF)
-            )
-            second_ref[strip, 0, rows, :] = jnp.where(
-                lower, rolled(joined[i], 48), rolled(joined[i + 4], 112)
+            out_ref[strip, 0, base + GROUP * i : base + GROUP * i + GROUP, :] = jnp.where(
+                lower, rolled(source[i], amounts[0]), rolled(source[i + 4], amounts[1])
             )
         here = after
 
 
-def spread(frame, shifts, n_rows, n_cols):
+def spread(exchange, frame, shifts, n_rows, n_cols):
     height, width = frame.shape
-    shape = lambda rows: jax.ShapeDtypeStruct((n_cols, n_rows, rows, LANES), jnp.float32)
-    block = lambda rows: pl.BlockSpec((n_cols, 1, rows, LANES), lambda band: (0, band, 0, 0))
-    first, second = pl.pallas_call(
-        spread_kernel,
+    rows = SECOND_ROWS if exchange else FIRST_ROWS
+    out = pl.pallas_call(
+        lambda *refs: spread_kernel(exchange, *refs),
         grid=(n_rows,),
-        out_shape=(shape(FIRST_ROWS), shape(SECOND_ROWS)),
+        out_shape=jax.ShapeDtypeStruct((n_cols, n_rows, rows, LANES), jnp.float32),
         in_specs=[pl.BlockSpec(memory_space=pltpu.HBM), pl.BlockSpec(memory_space=pltpu.HBM)],
-        out_specs=(block(FIRST_ROWS), block(SECOND_ROWS)),
+        out_specs=pl.BlockSpec((n_cols, 1, rows, LANES), lambda band: (0, band, 0, 0)),
         scratch_shapes=[
             pltpu.VMEM((height + 2 * REACH + GROUP, width), jnp.float32),
             pltpu.SMEM(shifts.shape, jnp.int32),
             pltpu.SemaphoreType.DMA((height // PATCH,)),
             pltpu.SemaphoreType.DMA,
         ],
-        compiler_params=pltpu.CompilerParams(vmem_limit_bytes=60 << 20),
-        name="spread",
+        compiler_params=pltpu.CompilerParams(vmem_limit_bytes=63 << 20),
+        name="spread_1" if exchange else "spread_0",
     )(shifts, frame)
-    peers = n_rows * n_cols
-    return (
-        first.reshape(peers, FIRST_ROWS, LANES),
-        second.reshape(peers, SECOND_ROWS, LANES),
-    )
+    return out.reshape(n_rows * n_cols, rows, LANES)
 
 
 def tile_copy(source, group, target, sem):
@@ -165,33 +160,26 @@
     return row
 
 
-def pack_kernel(first_ref, edge_ref, far_ref, tile, sems):
-    frames = first_ref.shape[0]
-    whole = pltpu.make_async_copy(first_ref.at[:, 0 : 2 * GROUP, :], edge_ref, sems.at[0])
-    whole.start()
-    copy = tile_copy(first_ref, 0, tile, sems.at[1])
+def far_kernel(first_ref, far_ref, tile, sem):
+    copy = tile_copy(first_ref, 0, tile, sem)
     copy.start()
     copy.wait()
     far_ref[...] = narrow_rows(tile, HALF + SHARED)
-    whole.wait()
-
-
-def pack(first):
+
+
+def far_rows(first):
     frames = first.shape[0]
     return pl.pallas_call(
-        pack_kernel,
-        out_shape=(
-            jax.ShapeDtypeStruct((frames, 2 * GROUP, LANES), jnp.float32),
-            jax.ShapeDtypeStruct((frames, LANES), jnp.float32),
-        ),
+        far_kernel,
+        out_shape=jax.ShapeDtypeStruct((frames, LANES), jnp.float32),
         in_specs=[pl.BlockSpec(memory_space=pltpu.HBM)],
-        out_specs=(pl.BlockSpec(memory_space=pltpu.VMEM),) * 2,
+        out_specs=pl.BlockSpec(memory_space=pltpu.VMEM),
         scratch_shapes=[
             pltpu.VMEM((frames * GROUP, LANES), jnp.float32),
-            pltpu.SemaphoreType.DMA((2,)),
+            pltpu.SemaphoreType.DMA,
         ],
-        compiler_params=pltpu.CompilerParams(vmem_limit_bytes=60 << 20),
-        name="pack",
+        compiler_params=pltpu.CompilerParams(vmem_limit_bytes=63 << 20),
+        name="far_rows",
     )(first)
 
 
@@ -261,7 +249,7 @@
         out_shape=jax.ShapeDtypeStruct(start.shape, jnp.float32),
         in_specs=[pl.BlockSpec(memory_space=pltpu.VMEM)],
         out_specs=pl.BlockSpec(memory_space=pltpu.VMEM),
-        compiler_params=pltpu.CompilerParams(vmem_limit_bytes=60 << 20),
+        compiler_params=pltpu.CompilerParams(vmem_limit_bytes=63 << 20),
         name="start_rows",
     )(start)
 
@@ -518,7 +506,7 @@
         in_specs=[pl.BlockSpec(memory_space=pltpu.SMEM)] + [hbm] * (len(operands) - 1),
         out_specs=tuple(out_specs),
         scratch_shapes=scratch,
-        compiler_params=pltpu.CompilerParams(vmem_limit_bytes=60 << 20),
+        compiler_params=pltpu.CompilerParams(vmem_limit_bytes=63 << 20),
         cost_estimate=pl.CostEstimate(
             flops=26 * 64 * 256 * PIXEL_ROWS * LANES,
             bytes_accessed=4 * frames * PIXEL_ROWS * LANES,
@@ -532,14 +520,15 @@
     n_rows = lax.axis_size("py")
     n_cols = lax.axis_size("px")
     odd = (lax.axis_index("py") & 1).astype(jnp.int32).reshape(1)
-    first, second = spread(frames[0], shifts, n_rows, n_cols)
+    first = spread(0, frames[0], shifts, n_rows, n_cols)
+    second = spread(1, frames[0], shifts, n_rows, n_cols)
     first = lax.all_to_all(first, ("px", "py"), split_axis=0, concat_axis=0, tiled=True)
-    first, start = lax.optimization_barrier((first, start_rows(start_basis.T)))
-    edge, far = pack(first)
+    first, start, second = lax.optimization_barrier((first, start_rows(start_basis.T), second))
+    across = [(i, i + 1 if i % 2 else i - 1) for i in range(1, n_rows - 1)]
+    far = lax.ppermute(far_rows(first), "py", across)
     pairs = [(i, i ^ 1) for i in range(n_rows)]
-    edge = lax.ppermute(edge, "py", pairs)
-    across = [(i, i + 1 if i % 2 else i - 1) for i in range(1, n_rows - 1)]
-    far = lax.ppermute(far, "py", across)
+    edge = lax.ppermute(first[:, : 2 * GROUP], "py", pairs)
+    far, second = lax.optimization_barrier((far, second))
     second = lax.all_to_all(second, ("px", "py"), split_axis=0, concat_axis=0, tiled=True)
     *left, next_means, next_movie, next_turned = decompose(0, odd, first, edge, far, start)
     spatial, background, bases = decompose(

time: 133 us -> 124 us (0.932); the launches traced: 131 us -> 123 us
  blocking collectives: 52.5 us -> 0 us
  waiting for transfers between devices: 15 us -> 41.3 us
  starting transfers between devices: 11.1 us -> 24.2 us
  Pallas kernels: 48.8 us -> 54.9 us
    all_to_all x1 -> x0, blocking collectives: 52.5 us -> none  [on_device(): lax.all_to_all(first, ('px', 'py'), split_axis=0, concat_axis=0, tiled=True)]
    all_to_all x0 -> x1, waiting for transfers between devices: none -> 30.9 us  [on_device(): lax.all_to_all(first, ('px', 'py'), split_axis=0, concat_axis=0, tiled=True)]
    all_to_all x0 -> x1, starting transfers between devices: none -> 11.9 us  [on_device(): lax.all_to_all(first, ('px', 'py'), split_axis=0, concat_axis=0, tiled=True)]
    ppermute x2, waiting for transfers between devices: 15 us -> 5.35 us  [the longest x1 3.06 us: on_device(): far = lax.ppermute(far_rows(first), 'py', across)]
    pallas_call x2 -> x3, Pallas kernels: 12.8 us -> 18.8 us  [the longest x2 17 us: spread(): pl.pallas_call(lambda *refs: spread_kernel(exchange, *refs), grid=(n_rows...]
    all_to_all x1, waiting for transfers between devices: 0.01 us -> 5.05 us  [on_device(): lax.all_to_all(second, ('px', 'py'), split_axis=0, concat_axis=0, tiled=T...]
    unnamed x6 -> x4, local copies, waits for them, and re-layouts: 2.41 us -> 1 us
    all_to_all x1, starting transfers between devices: 5.47 us -> 6.83 us  [on_device(): lax.all_to_all(second, ('px', 'py'), split_axis=0, concat_axis=0, tiled=T...]
  transfers between devices with their start and end apart: 3 -> 4, of which waited for: 1 -> 4; matrix products, arithmetic and copies ran while one was open for 0% -> 1% of each run, Pallas kernels for 17% -> 23%
where the time goes in v3:
time: 124 us; the launch traced here: 123 us
  Pallas kernels  54.9 us (44%)
  waiting for transfers between devices  41.3 us (33%)
  starting transfers between devices  24.2 us (20%)
  local copies, waits for them, and re-layouts  2.32 us (2%)
    pallas_call x2, Pallas kernels, decompose(): pl.pallas_call(patch_1_kernel if patch else patch_0_kernel, out_shape=tup...  34.3 us
    all_to_all x1, waiting for transfers between devices, on_device(): lax.all_to_all(first, ('px', 'py'), split_axis=0, concat_axis=0, tiled=True)  30.9 us
    pallas_call x2, Pallas kernels, spread(): pl.pallas_call(lambda *refs: spread_kernel(exchange, *refs), grid=(n_rows...  17 us
    all_to_all x1, starting transfers between devices, on_device(): lax.all_to_all(first, ('px', 'py'), split_axis=0, concat_axis=0, tiled=True)  11.9 us
    all_to_all x1, starting transfers between devices, on_device(): lax.all_to_all(second, ('px', 'py'), split_axis=0, concat_axis=0, tiled=T...  6.83 us
    all_to_all x1, waiting for transfers between devices, on_device(): lax.all_to_all(second, ('px', 'py'), split_axis=0, concat_axis=0, tiled=T...  5.05 us
    ppermute x1, starting transfers between devices, on_device(): far = lax.ppermute(far_rows(first), 'py', across)  4.23 us
    ppermute x1, waiting for transfers between devices, on_device(): far = lax.ppermute(far_rows(first), 'py', across)  3.06 us
  transfers between devices with their start and end apart: 4, of which 4 were waited for; matrix products, arithmetic and copies ran while one was open for 1% of the time, Pallas kernels for 23%

profile of v3, /device:TPU:1, one launch (start us, length us, event | category | flops | bytes accessed | tf_op | source)
XLA Modules:
  0.0 123.3 jit_solution(992061607863524744)
XLA Ops:
  0.6 9.0 %spread_0.1 = f32[8,16,48,128]{3,2,1,0:T(8,128)} custom-call(s32[1,2]{1,0:T(1,128)} %refs_0_.3, f32[1024,1024]{1,0:T(8,128)} %bitcast.8), custom_call_target="tpu_custom_call" | custom-call | tf_op jit(solution)/shard_map/spread_0/pallas_call | solution.py:125
  9.6 11.9 %all-to-all-start = ((f32[128,48,128]{2,1,0:T(8,128)}), f32[128,48,128]{2,1,0:T(8,128)}, u32[]{:S(2)}, u32[]{:S(2)}) async-start(f32[128,48,128]{2,1,0:T(8,128)} %bitcast.10), calls=%async_computation | async-start | bytes 6291456 | tf_op jit(solution)/shard_map/all_to_all | solution.py:525
  21.5 8.0 %spread_1.1 = f32[8,16,32,128]{3,2,1,0:T(8,128)} custom-call(s32[1,2]{1,0:T(1,128)} %refs_0_.3, f32[1024,1024]{1,0:T(8,128)} %bitcast.9), custom_call_target="tpu_custom_call" | custom-call | tf_op jit(solution)/shard_map/spread_1/pallas_call | solution.py:125
  29.5 1.8 %start_rows.1.start_ref = f32[16,128]{1,0:T(8,128)} custom-call(f32[16,128]{1,0:T(8,128)} %bitcast.12), custom_call_target="tpu_custom_call" | custom-call | tf_op jit(solution)/shard_map/start_rows/pallas_call | solution.py:247
  31.3 30.9 %all-to-all-done.first_ref = f32[128,48,128]{2,1,0:T(8,128)} async-done(((f32[128,48,128]{2,1,0:T(8,128)}), f32[128,48,128]{2,1,0:T(8,128)}, u32[]{:S(2)}, u32[]{:S(2)}) %all-to-all-start) | async-done | bytes 3145760 | tf_op jit(solution)/shard_map/all_to_all | solution.py:525
  62.2 1.9 %far_rows.1 = f32[128,128]{1,0:T(8,128)} custom-call(f32[128,48,128]{2,1,0:T(8,128)} %all-to-all-done.first_ref), custom_call_target="tpu_custom_call" | custom-call | tf_op jit(solution)/shard_map/far_rows/pallas_call | solution.py:172
  64.0 4.2 %collective-permute-start = (f32[128,128]{1,0:T(8,128)}, f32[128,128]{1,0:T(8,128)S(1)}, u32[]{:S(2)}, u32[]{:S(2)}) collective-permute-start(f32[128,128]{1,0:T(8,128)} %far_rows.1), channel_id=1, source_target_pairs={{8,16},{16,8},{24,32},{32,24},{40,48},{48,40},{56,64},{64,56},{72,... | collective-permute-start | bytes 196616 | tf_op jit(solution)/shard_map/ppermute | solution.py:528
  68.3 3.1 %collective-permute-done.far_ref = f32[128,128]{1,0:T(8,128)S(1)} collective-permute-done((f32[128,128]{1,0:T(8,128)}, f32[128,128]{1,0:T(8,128)S(1)}, u32[]{:S(2)}, u32[]{:S(2)}) %collective-permute-start) | collective-permute-done | bytes 65568 | tf_op jit(solution)/shard_map/ppermute | solution.py:528
  71.3 0.0 copy-start.1
  71.3 6.8 %all-to-all-start.1 = ((f32[128,32,128]{2,1,0:T(8,128)}), f32[128,32,128]{2,1,0:T(8,128)}, u32[]{:S(2)}, u32[]{:S(2)}) async-start(f32[128,32,128]{2,1,0:T(8,128)} %bitcast.11), calls=%async_computation.1 | async-start | bytes 4194304 | tf_op jit(solution)/shard_map/all_to_all | solution.py:532
  78.2 1.3 %slice.3 = f32[128,16,128]{2,1,0:T(8,128)S(1)} slice(f32[128,48,128]{2,1,0:T(8,128)} %all-to-all-done.first_ref), slice={[0:128], [0:16], [0:128]} | slice | bytes 2097152 | tf_op jit(solution)/shard_map/slice | solution.py:530
  79.5 0.0 copy-done.1
  79.5 1.2 collective-permute-start.1
  80.7 2.3 %collective-permute-done.1.edge_ref = f32[128,16,128]{2,1,0:T(8,128)S(1)} collective-permute-done((f32[128,16,128]{2,1,0:T(8,128)S(1)}, f32[128,16,128]{2,1,0:T(8,128)S(1)}, u32[]{:S(2)}, u32[]{:S(2)}) %collective-permute-start.1) | collective-permute-done | bytes 1048608 | tf_op jit(solution)/shard_map/ppermute | solution.py:530
  83.0 0.0 copy-start
  83.0 1.0 copy-done
  84.0 18.3 %patch_0.1 = (f32[16,64,128]{2,1,0:T(8,128)}, f32[64,128]{1,0:T(8,128)}, f32[16,128]{1,0:T(8,128)}, f32[24,128]{1,0:T(8,128)}, bf16[256,2304]{1,0:T(8,128)(2,1)}, /*index=5*/bf16[2304,256]{1,0:T(8,128)(2,1)}) custom-call(s32[1]{0:T(128)} %bitcast.odd_ref, f32[128,48,128]{2,1,0:T(8,128)} %all-to-all-done.first_ref, f32[128,16,128]{2,1,0:T(8,128)} %copy-done, ...), custom_call_target="tpu_custom_call" | custom-call | flops 2726297600 | bytes 3276800 | tf_op jit(solution)/shard_map/patch_0/pallas_call | solution.py:503
  102.3 5.1 %all-to-all-done.1.second_ref = f32[128,32,128]{2,1,0:T(8,128)} async-done(((f32[128,32,128]{2,1,0:T(8,128)}), f32[128,32,128]{2,1,0:T(8,128)}, u32[]{:S(2)}, u32[]{:S(2)}) %all-to-all-start.1) | async-done | bytes 2097184 | tf_op jit(solution)/shard_map/all_to_all | solution.py:532
  107.3 16.0 %patch_1.1 = (f32[16,64,128]{2,1,0:T(8,128)}, f32[64,128]{1,0:T(8,128)}, f32[2,16,128]{2,1,0:T(8,128)}) custom-call(s32[1]{0:T(128)} %bitcast.odd_ref, f32[128,32,128]{2,1,0:T(8,128)} %all-to-all-done.1.second_ref, bf16[256,2304]{1,0:T(8,128)(2,1)} %get-tuple-element.22.next_movie_in, bf16[2304,256]{1,0:T(8,128)(2,1)} %get-tuple-element.23.next_turned_in, ...), custom_call_target="tpu_custom_call" | custom-call | flops 2726297600 | bytes 3276800 | tf_op jit(solution)/shard_map/patch_1/pallas_call | solution.py:503
Async XLA Ops:
  9.6 52.5 %all-to-all-start = ((f32[128,48,128]{2,1,0:T(8,128)}), f32[128,48,128]{2,1,0:T(8,128)}, u32[]{:S(2)}, u32[]{:S(2)}) async-start(f32[128,48,128]{2,1,0:T(8,128)} %bitcast.10), calls=%async_computation | async-start | bytes 6291456 | tf_op jit(solution)/shard_map/all_to_all | solution.py:525
  64.0 7.3 %collective-permute-start = (f32[128,128]{1,0:T(8,128)}, f32[128,128]{1,0:T(8,128)S(1)}, u32[]{:S(2)}, u32[]{:S(2)}) collective-permute-start(f32[128,128]{1,0:T(8,128)} %far_rows.1), channel_id=1, source_target_pairs={{8,16},{16,8},{24,32},{32,24},{40,48},{48,40},{56,64},{64,56},{72,... | collective-permute-start | bytes 196616 | tf_op jit(solution)/shard_map/ppermute | solution.py:528
  71.3 8.2 %copy-start.1 = (f32[128,128]{1,0:T(8,128)}, f32[128,128]{1,0:T(8,128)S(1)}, u32[]{:S(2)}) copy-start(f32[128,128]{1,0:T(8,128)S(1)} %collective-permute-done.far_ref) | copy-start | bytes 196612
  71.3 36.0 %all-to-all-start.1 = ((f32[128,32,128]{2,1,0:T(8,128)}), f32[128,32,128]{2,1,0:T(8,128)}, u32[]{:S(2)}, u32[]{:S(2)}) async-start(f32[128,32,128]{2,1,0:T(8,128)} %bitcast.11), calls=%async_computation.1 | async-start | bytes 4194304 | tf_op jit(solution)/shard_map/all_to_all | solution.py:532
  79.5 3.5 %collective-permute-start.1 = (f32[128,16,128]{2,1,0:T(8,128)S(1)}, f32[128,16,128]{2,1,0:T(8,128)S(1)}, u32[]{:S(2)}, u32[]{:S(2)}) collective-permute-start(f32[128,16,128]{2,1,0:T(8,128)S(1)} %slice.3), channel_id=1, source_target_pairs={{0,8},{8,0},{16,24},{24,16},{32,40},{40,32},{48,56},{56,48},{64,72... | collective-permute-start | bytes 3145736 | tf_op jit(solution)/shard_map/ppermute | solution.py:530
  83.0 1.0 copy-start

commit v4 on v3

--- a/solution.py
+++ b/solution.py
@@ -18,17 +18,18 @@
 GROUP = 8
 HALF = 64
 SHARED = 16
-FIRST_ROWS = 48
+FIRST_ROWS = 56
 UNROLL = 4
 SECOND_ROWS = 32
 
+POSITIONS = 10
+
 
 def lane_ids(shape):
     return lax.broadcasted_iota(jnp.int32, shape, len(shape) - 1)
 
 
-def spread_kernel(exchange, shifts_hbm, frame_ref, out_ref, padded, shifts_ref, sems, shift_sem):
-    band = pl.program_id(0)
+def spread_kernel(exchange, shifts_hbm, frame_ref, out_ref, padded, staged, shifts_ref, sems):
     height, width = frame_ref.shape
     bands = height // PATCH
     strips = width // LANES
@@ -41,98 +42,111 @@
             sems.at[chunk],
         )
 
-    @pl.when(band == 0)
-    def _():
-        shift_copy = pltpu.make_async_copy(shifts_hbm, shifts_ref, shift_sem)
-        shift_copy.start()
-        for chunk in range(bands):
-            rows_in(chunk).start()
-        padded[0:REACH, :] = jnp.zeros((REACH, width), jnp.float32)
-        padded[REACH + height :, :] = jnp.zeros((REACH + GROUP, width), jnp.float32)
-        shift_copy.wait()
-        rows_in(0).wait()
-
-    @pl.when(band < bands - 1)
-    def _():
-        rows_in(band + 1).wait()
-
-    odd = band % 2
-    row0 = band * PATCH + MARGIN * (1 + odd) - shifts_ref[0, 0]
-    tile0 = row0 // GROUP * GROUP
-    rest = row0 % GROUP
-    starts = [
-        pl.multiple_of(tile0 + GROUP * jnp.where(odd == 0, p, 8 - p), GROUP) for p in range(9)
-    ]
-    margin_inside = (band > 0) & (band < bands - 1)
-    margin_inside = margin_inside.astype(jnp.int32)
+    def band_out(band):
+        return pltpu.make_async_copy(
+            staged.at[:, band], out_ref.at[:, band], sems.at[bands + band]
+        )
+
+    shift_copy = pltpu.make_async_copy(shifts_hbm, shifts_ref, sems.at[2 * bands])
+    shift_copy.start()
+    for chunk in range(bands):
+        rows_in(chunk).start()
+    padded[0:REACH, :] = jnp.zeros((REACH, width), jnp.float32)
+    padded[REACH + height :, :] = jnp.zeros((REACH + GROUP, width), jnp.float32)
+    shift_copy.wait()
+    rows_in(0).wait()
     turn = MARGIN + shifts_ref[0, 1]
     shape = (GROUP, LANES)
     lane = lane_ids(shape)
     lower = lane < HALF
-    from_above = lax.broadcasted_iota(jnp.int32, shape, 0) >= rest
     from_here = lane < LANES - turn
     landing = (lane + turn) % LANES
     to_next = landing < 16
-    zeros = jnp.zeros(shape, jnp.float32)
-
-    def rows_of(strip):
-        lanes = slice(strip * LANES, (strip + 1) * LANES)
-        tiles = []
-        for p in range(9):
-            pair = padded[pl.ds(starts[p], 2 * GROUP), lanes]
-            tile = jnp.where(from_above, pair[:GROUP], pair[GROUP:])
-            tile = pltpu.roll(tile, GROUP - rest, 0)
-            if p == 0:
-                tile = jnp.where(margin_inside > 0, tile, 0.0)
-            tiles.append(tile)
-        return tiles
+    needed = POSITIONS if exchange == 0 else 8
 
     def rolled(tile, amount):
         return pltpu.roll(tile, (turn + amount) % LANES, 1)
 
-    before = rows_of(0)
-    here = [jnp.where(from_here & (landing >= MARGIN), tile, 0.0) for tile in before]
-    for strip in range(strips):
-        if strip + 1 < strips:
-            following = rows_of(strip + 1)
-            after = [jnp.where(from_here, n, b) for n, b in zip(following, before)]
-            before = following
-        else:
-            after = [jnp.where(from_here | (landing >= MARGIN), 0.0, b) for b in before]
-        joined = [jnp.where(to_next, a, h) for a, h in zip(after, here)]
-        if exchange == 0:
-            tile = rolled(here[8], 0)
-            for p in (1, 2, 3):
-                tile = jnp.where(lane >= HALF + SHARED * p, rolled(here[p], SHARED * p), tile)
-            out_ref[strip, 0, 0:8, :] = tile
-            tile = rolled(joined[8], 48)
-            for p in (4, 5, 6, 7):
-                tile = jnp.where(lane >= SHARED * p, rolled(here[p], SHARED * (p - 4)), tile)
-            out_ref[strip, 0, 8:16, :] = tile
-            source, amounts, base = here, (0, HALF), 2 * GROUP
-        else:
-            source, amounts, base = joined, (48, 112), 0
-        for i in range(4):
-            out_ref[strip, 0, base + GROUP * i : base + GROUP * i + GROUP, :] = jnp.where(
-                lower, rolled(source[i], amounts[0]), rolled(source[i + 4], amounts[1])
-            )
-        here = after
+    @pl.loop(0, bands)
+    def _(band):
+        @pl.when(band < bands - 1)
+        def _():
+            rows_in(band + 1).wait()
+
+        odd = band % 2
+        row0 = band * PATCH + MARGIN - shifts_ref[0, 0]
+        tile0 = row0 // GROUP * GROUP
+        rest = row0 % GROUP
+        starts = [
+            pl.multiple_of(tile0 + GROUP * jnp.where(odd == 0, p, POSITIONS - 1 - p), GROUP)
+            for p in range(needed)
+        ]
+        margin_inside = ((band > 0) & (band < bands - 1)).astype(jnp.int32)
+        from_above = lax.broadcasted_iota(jnp.int32, shape, 0) >= rest
+
+        def rows_of(strip):
+            lanes = slice(strip * LANES, (strip + 1) * LANES)
+            tiles = []
+            for p in range(needed):
+                pair = padded[pl.ds(starts[p], 2 * GROUP), lanes]
+                tile = jnp.where(from_above, pair[:GROUP], pair[GROUP:])
+                tile = pltpu.roll(tile, GROUP - rest, 0)
+                if p == 0:
+                    tile = jnp.where(margin_inside > 0, tile, 0.0)
+                tiles.append(tile)
+            return tiles
+
+        before = rows_of(0)
+        here = [jnp.where(from_here & (landing >= MARGIN), tile, 0.0) for tile in before]
+        for strip in range(strips):
+            if strip + 1 < strips:
+                following = rows_of(strip + 1)
+                after = [jnp.where(from_here, n, b) for n, b in zip(following, before)]
+                before = following
+            else:
+                after = [jnp.where(from_here | (landing >= MARGIN), 0.0, b) for b in before]
+            joined = [jnp.where(to_next, a, h) for a, h in zip(after, here)]
+            if exchange == 0:
+                tile = rolled(here[8], 0)
+                for p in (1, 2, 3):
+                    tile = jnp.where(lane >= HALF + SHARED * p, rolled(here[p], SHARED * p), tile)
+                staged[strip, band, 0:8, :] = tile
+                tile = rolled(joined[8], 48)
+                for p in (4, 5, 6, 7):
+                    tile = jnp.where(lane >= SHARED * p, rolled(here[p], SHARED * (p - 4)), tile)
+                staged[strip, band, 8:16, :] = tile
+                tile = jnp.where(lane < HALF + SHARED, rolled(here[9], 0), rolled(here[0], SHARED))
+                tile = jnp.where(lane < HALF + 2 * SHARED, tile, 0.0)
+                staged[strip, band, 48:56, :] = tile
+                source, amounts, base = here, (0, HALF), 2 * GROUP
+            else:
+                source, amounts, base = joined, (48, 112), 0
+            for i in range(4):
+                staged[strip, band, base + GROUP * i : base + GROUP * i + GROUP, :] = jnp.where(
+                    lower, rolled(source[i], amounts[0]), rolled(source[i + 4], amounts[1])
+                )
+            here = after
+        band_out(band).start()
+
+    for band in range(bands):
+        band_out(band).wait()
 
 
 def spread(exchange, frame, shifts, n_rows, n_cols):
     height, width = frame.shape
     rows = SECOND_ROWS if exchange else FIRST_ROWS
+    shape = (n_cols, n_rows, rows, LANES)
+    hbm = pl.BlockSpec(memory_space=pltpu.HBM)
     out = pl.pallas_call(
         lambda *refs: spread_kernel(exchange, *refs),
-        grid=(n_rows,),
-        out_shape=jax.ShapeDtypeStruct((n_cols, n_rows, rows, LANES), jnp.float32),
-        in_specs=[pl.BlockSpec(memory_space=pltpu.HBM), pl.BlockSpec(memory_space=pltpu.HBM)],
-        out_specs=pl.BlockSpec((n_cols, 1, rows, LANES), lambda band: (0, band, 0, 0)),
+        out_shape=jax.ShapeDtypeStruct(shape, jnp.float32),
+        in_specs=[hbm, hbm],
+        out_specs=hbm,
         scratch_shapes=[
             pltpu.VMEM((height + 2 * REACH + GROUP, width), jnp.float32),
+            pltpu.VMEM(shape, jnp.float32),
             pltpu.SMEM(shifts.shape, jnp.int32),
-            pltpu.SemaphoreType.DMA((height // PATCH,)),
-            pltpu.SemaphoreType.DMA,
+            pltpu.SemaphoreType.DMA((2 * (height // PATCH) + 1,)),
         ],
         compiler_params=pltpu.CompilerParams(vmem_limit_bytes=63 << 20),
         name="spread_1" if exchange else "spread_0",
@@ -158,29 +172,6 @@
         values = pltpu.roll(values, (SHARED * s - lane0) % LANES, 1)
         row = jnp.where(lane >= SHARED * s, values, row)
     return row
-
-
-def far_kernel(first_ref, far_ref, tile, sem):
-    copy = tile_copy(first_ref, 0, tile, sem)
-    copy.start()
-    copy.wait()
-    far_ref[...] = narrow_rows(tile, HALF + SHARED)
-
-
-def far_rows(first):
-    frames = first.shape[0]
-    return pl.pallas_call(
-        far_kernel,
-        out_shape=jax.ShapeDtypeStruct((frames, LANES), jnp.float32),
-        in_specs=[pl.BlockSpec(memory_space=pltpu.HBM)],
-        out_specs=pl.BlockSpec(memory_space=pltpu.VMEM),
-        scratch_shapes=[
-            pltpu.VMEM((frames * GROUP, LANES), jnp.float32),
-            pltpu.SemaphoreType.DMA,
-        ],
-        compiler_params=pltpu.CompilerParams(vmem_limit_bytes=63 << 20),
-        name="far_rows",
-    )(first)
 
 
 def split(values):
@@ -315,8 +306,8 @@
             shared, at = (5, SHARED * p) if 4 <= p < 8 else (4, HALF + SHARED * (p % 8))
             from_own = lane < HALF - MARGIN
         else:
-            tile, turn = (5, HALF + MARGIN) if p == 8 else (p % 4, HALF + MARGIN - HALF * (p // 4))
-            shared, at = 4, SHARED * (p % 8)
+            tile, turn = (4, HALF + MARGIN) if p == 8 else (p % 4, HALF + MARGIN - HALF * (p // 4))
+            shared, at = 5, SHARED * (p % 8)
             from_own = lane >= HALF + MARGIN
         own = pltpu.roll(tiles[tile], turn % LANES, 1)
         both = pltpu.roll(tiles[shared], (HALF - MARGIN - at) % LANES, 1)
@@ -365,23 +356,23 @@
 
 
 PIXEL_ROWS = EDGE * EDGE // LANES
-NEXT_ROWS = PIXEL_ROWS - SECOND_ROWS
-
-
-def patch_0_kernel(odd_ref, first_ref, edge_ref, far_ref, start_ref, *refs):
+NEXT_ROWS = 10
+
+
+def patch_0_kernel(odd_ref, first_ref, start_ref, *refs):
     spatial_ref, mean_ref, basis_ref, next_means, next_movie_out, next_turned_out = refs[:6]
-    raw, far, start, movie, turned, next_movie, next_turned = refs[6:13]
-    means, projected, packed, sems = refs[13:]
+    raw, start, movie, turned, next_movie, next_turned = refs[6:12]
+    means, projected, packed, sems = refs[12:]
     frames = first_ref.shape[0]
-    sources = [(first_ref, g) for g in (2, 3, 4, 5, 0, 1)] + [(edge_ref, 0), (edge_ref, 1)]
-    copies = [tile_copy(ref, g, raw.at[i], sems.at[i]) for i, (ref, g) in enumerate(sources)]
-    copies.append(pltpu.make_async_copy(far_ref, far, sems.at[8]))
-    copies.append(pltpu.make_async_copy(start_ref, start, sems.at[9]))
+    copies = [
+        tile_copy(first_ref, g, raw.at[i], sems.at[i]) for i, g in enumerate((2, 3, 4, 5, 0, 1, 6))
+    ]
+    copies.append(pltpu.make_async_copy(start_ref, start, sems.at[7]))
     for copy in copies:
         copy.start()
     results = [
-        pltpu.make_async_copy(next_movie, next_movie_out, sems.at[10]),
-        pltpu.make_async_copy(next_turned, next_turned_out, sems.at[11]),
+        pltpu.make_async_copy(next_movie, next_movie_out, sems.at[8]),
+        pltpu.make_async_copy(next_turned, next_turned_out, sems.at[9]),
     ]
 
     def read(i, s):
@@ -404,14 +395,12 @@
         keep_row(40 + s, jnp.where(lower, read(6, s), edge), movie, turned, means)
         both = jnp.where(lower, pltpu.roll(read(4, s), HALF, 1), edge)
         keep_row(s, both, next_movie, next_turned, next_means)
-        both = jnp.where(lower, edge, pltpu.roll(read(7, s), HALF, 1))
-        keep_row(GROUP + s, both, next_movie, next_turned, next_means)
 
     once = (odd_ref[0] >= 0).astype(jnp.int32)
-    near = narrow_rows(raw.at[6], HALF)
-    for row, values in ((0, near), (1, far[...])):
+    for row in range(2):
+        values = narrow_rows(raw.at[6], HALF + SHARED * row)
         keep_row(48 + row, values, movie, turned, means)
-        keep_row(2 * GROUP + row, values, next_movie, next_turned, next_means)
+        keep_row(GROUP + row, values, next_movie, next_turned, next_means)
     for copy in results:
         copy.start()
     basis, level = iterate(start[...], movie, turned, projected, frames, once)
@@ -422,34 +411,54 @@
 
 
 def patch_1_kernel(
-    odd_ref, second_ref, next_movie_in, next_turned_in, next_means_in, start_ref, *refs
+    odd_ref,
+    second_ref,
+    first_ref,
+    edge_ref,
+    next_movie_in,
+    next_turned_in,
+    next_means_in,
+    start_ref,
+    *refs,
 ):
     earlier_in, outs = refs[:3], refs[3:6]
     raw, start, next_means = refs[6:9]
     earlier = refs[9:12]
     movie, turned, means, projected, packed, sems = refs[12:]
-    own = SECOND_ROWS * LANES
+    done = PIXEL_ROWS - NEXT_ROWS
+    own = done * LANES
     frames = second_ref.shape[0]
     tiles = SECOND_ROWS // GROUP
-    copies = [tile_copy(second_ref, i, raw.at[i], sems.at[i]) for i in range(tiles)]
+    sources = [(second_ref, i) for i in range(tiles)] + [(first_ref, 1), (edge_ref, 0)]
+    copies = [tile_copy(ref, g, raw.at[i], sems.at[i]) for i, (ref, g) in enumerate(sources)]
     sources = (next_movie_in, next_turned_in, next_means_in, start_ref, *earlier_in)
     targets = (movie.at[:, own:], turned.at[own:, :], next_means, start, *earlier)
-    for i, (source, target) in enumerate(zip(sources, targets)):
-        copies.append(pltpu.make_async_copy(source, target, sems.at[tiles + i]))
+    for source, target in zip(sources, targets):
+        copies.append(pltpu.make_async_copy(source, target, sems.at[len(copies)]))
     for copy in copies:
         copy.start()
+
+    def read(i, s):
+        return raw[i, pl.ds(s, frames, stride=GROUP), :]
+
     for i in range(tiles):
         copies[i].wait()
 
         @pl.loop(0, GROUP, unroll=UNROLL)
         def _(s, i=i):
-            values = raw[i, pl.ds(s, frames, stride=GROUP), :]
-            keep_row(GROUP * i + s, values, movie, turned, means)
+            keep_row(GROUP * i + s, read(i, s), movie, turned, means)
 
     for copy in copies[tiles:]:
         copy.wait()
+    lower = lane_ids((frames, LANES)) < HALF
+
+    @pl.loop(0, GROUP, unroll=UNROLL)
+    def _(s):
+        both = jnp.where(lower, read(tiles, s), pltpu.roll(read(tiles + 1, s), HALF, 1))
+        keep_row(SECOND_ROWS + s, both, movie, turned, means)
+
     once = (odd_ref[0] >= 0).astype(jnp.int32)
-    means[SECOND_ROWS : SECOND_ROWS + 2 * GROUP, :] = next_means[0 : 2 * GROUP, :]
+    means[done : done + GROUP, :] = next_means[0:GROUP, :]
     basis, level = iterate(start[...], movie, turned, projected, frames, once)
     finish(1, odd_ref[0], basis, level, means, projected, packed, outs, earlier)
 
@@ -472,33 +481,30 @@
     ]
     out_specs = [vmem] * 3
     start = pltpu.VMEM((RANK, frames), jnp.float32)
-    next_means = (24, LANES)
+    next_means = (16, LANES)
     if patch == 0:
         shapes.append(jax.ShapeDtypeStruct(next_means, jnp.float32))
         shapes += parts(NEXT_ROWS, jax.ShapeDtypeStruct)
         out_specs += [vmem, hbm, hbm]
         scratch = [
-            pltpu.VMEM((8, frames * GROUP, LANES), jnp.float32),
-            pltpu.VMEM((frames, LANES), jnp.float32),
+            pltpu.VMEM((7, frames * GROUP, LANES), jnp.float32),
             start,
             *parts(PIXEL_ROWS, pltpu.VMEM),
             *parts(NEXT_ROWS, pltpu.VMEM),
         ]
     else:
         scratch = [
-            pltpu.VMEM((SECOND_ROWS // GROUP, frames * GROUP, LANES), jnp.float32),
+            pltpu.VMEM((6, frames * GROUP, LANES), jnp.float32),
             start,
             pltpu.VMEM(next_means, jnp.float32),
-            pltpu.VMEM(operands[6].shape, jnp.float32),
-            pltpu.VMEM(operands[7].shape, jnp.float32),
-            pltpu.VMEM(operands[8].shape, jnp.float32),
+            *(pltpu.VMEM(value.shape, jnp.float32) for value in operands[-3:]),
             *parts(PIXEL_ROWS, pltpu.VMEM),
         ]
     scratch += [
         pltpu.VMEM((56, LANES), jnp.float32),
         pltpu.VMEM((RANK, PIXEL_ROWS * LANES), jnp.float32),
         pltpu.VMEM((RANK * 48, LANES), jnp.float32),
-        pltpu.SemaphoreType.DMA((12,)),
+        pltpu.SemaphoreType.DMA((13,)),
     ]
     return pl.pallas_call(
         patch_1_kernel if patch else patch_0_kernel,
@@ -524,15 +530,12 @@
     second = spread(1, frames[0], shifts, n_rows, n_cols)
     first = lax.all_to_all(first, ("px", "py"), split_axis=0, concat_axis=0, tiled=True)
     first, start, second = lax.optimization_barrier((first, start_rows(start_basis.T), second))
-    across = [(i, i + 1 if i % 2 else i - 1) for i in range(1, n_rows - 1)]
-    far = lax.ppermute(far_rows(first), "py", across)
     pairs = [(i, i ^ 1) for i in range(n_rows)]
-    edge = lax.ppermute(first[:, : 2 * GROUP], "py", pairs)
-    far, second = lax.optimization_barrier((far, second))
+    edge = lax.ppermute(first[:, GROUP : 2 * GROUP], "py", pairs)
     second = lax.all_to_all(second, ("px", "py"), split_axis=0, concat_axis=0, tiled=True)
-    *left, next_means, next_movie, next_turned = decompose(0, odd, first, edge, far, start)
+    *left, next_means, next_movie, next_turned = decompose(0, odd, first, start)
     spatial, background, bases = decompose(
-        1, odd, second, next_movie, next_turned, next_means, start, *left
+        1, odd, second, first, edge, next_movie, next_turned, next_means, start, *left
     )
     return (spatial, bases.swapaxes(1, 2)[None], background)
 

time: 124 us -> 117 us (0.944)
  Pallas kernels: 54.9 us -> 46.8 us
  waiting for transfers between devices: 41.3 us -> 49.3 us
  starting transfers between devices: 24.2 us -> 19.1 us
    all_to_all x1, waiting for transfers between devices: 30.9 us -> 40.2 us  [on_device(): lax.all_to_all(first, ('px', 'py'), split_axis=0, concat_axis=0, tiled=True)]
    pallas_call x3 -> x2, Pallas kernels: 18.8 us -> 10.7 us  [spread(): pl.pallas_call(lambda *refs: spread_kernel(exchange, *refs), out_shape=ja...]
    ppermute x2 -> x1, waiting for transfers between devices: 5.35 us -> 0.01 us  [on_device(): edge = lax.ppermute(first[:, GROUP:2 * GROUP], 'py', pairs)]
    ppermute x2 -> x1, starting transfers between devices: 5.45 us -> 1.22 us  [on_device(): edge = lax.ppermute(first[:, GROUP:2 * GROUP], 'py', pairs)]
    all_to_all x1, waiting for transfers between devices: 5.05 us -> 9.12 us  [on_device(): lax.all_to_all(second, ('px', 'py'), split_axis=0, concat_axis=0, tiled=T...]
  transfers between devices with their start and end apart: 4 -> 3, of which waited for: 4 -> 2; matrix products, arithmetic and copies ran while one was open for 1% -> 1% of each run, Pallas kernels for 23% -> 21%
where the time goes in v4:
time: 117 us
  waiting for transfers between devices  49.3 us (42%)
  Pallas kernels  46.8 us (40%)
  starting transfers between devices  19.1 us (16%)
    all_to_all x1, waiting for transfers between devices, on_device(): lax.all_to_all(first, ('px', 'py'), split_axis=0, concat_axis=0, tiled=True)  40.2 us
    pallas_call x2, Pallas kernels, decompose(): pl.pallas_call(patch_1_kernel if patch else patch_0_kernel, out_shape=tup...  34.3 us
    all_to_all x1, starting transfers between devices, on_device(): lax.all_to_all(first, ('px', 'py'), split_axis=0, concat_axis=0, tiled=True)  11.9 us
    pallas_call x2, Pallas kernels, spread(): pl.pallas_call(lambda *refs: spread_kernel(exchange, *refs), out_shape=ja...  10.7 us
    all_to_all x1, waiting for transfers between devices, on_device(): lax.all_to_all(second, ('px', 'py'), split_axis=0, concat_axis=0, tiled=T...  9.12 us
    all_to_all x1, starting transfers between devices, on_device(): lax.all_to_all(second, ('px', 'py'), split_axis=0, concat_axis=0, tiled=T...  5.94 us
  transfers between devices with their start and end apart: 3, of which 2 were waited for; matrix products, arithmetic and copies ran while one was open for 1% of the time, Pallas kernels for 21%

profile of v4, /device:TPU:1, one launch (start us, length us, event | category | flops | bytes accessed | tf_op | source)
XLA Modules:
  0.0 116.9 jit_solution(10218084485183144592)
XLA Ops:
  0.6 6.2 %spread_0.1 = f32[8,16,56,128]{3,2,1,0:T(8,128)} custom-call(s32[1,2]{1,0:T(1,128)} %refs_0_.3, f32[1024,1024]{1,0:T(8,128)} %bitcast.8), custom_call_target="tpu_custom_call" | custom-call | tf_op jit(solution)/shard_map/spread_0/pallas_call | solution.py:140
  6.8 11.9 %all-to-all-start = ((f32[128,56,128]{2,1,0:T(8,128)}), f32[128,56,128]{2,1,0:T(8,128)}, u32[]{:S(2)}, u32[]{:S(2)}) async-start(f32[128,56,128]{2,1,0:T(8,128)} %bitcast.10), calls=%async_computation | async-start | bytes 7340032 | tf_op jit(solution)/shard_map/all_to_all | solution.py:531
  18.7 4.5 %spread_1.1 = f32[8,16,32,128]{3,2,1,0:T(8,128)} custom-call(s32[1,2]{1,0:T(1,128)} %refs_0_.3, f32[1024,1024]{1,0:T(8,128)} %bitcast.9), custom_call_target="tpu_custom_call" | custom-call | tf_op jit(solution)/shard_map/spread_1/pallas_call | solution.py:140
  23.3 1.8 %start_rows.1.start_ref = f32[16,128]{1,0:T(8,128)} custom-call(f32[16,128]{1,0:T(8,128)} %bitcast.12), custom_call_target="tpu_custom_call" | custom-call | tf_op jit(solution)/shard_map/start_rows/pallas_call | solution.py:238
  25.0 40.2 %all-to-all-done.first_ref = f32[128,56,128]{2,1,0:T(8,128)} async-done(((f32[128,56,128]{2,1,0:T(8,128)}), f32[128,56,128]{2,1,0:T(8,128)}, u32[]{:S(2)}, u32[]{:S(2)}) %all-to-all-start) | async-done | bytes 3670048 | tf_op jit(solution)/shard_map/all_to_all | solution.py:531
  65.2 5.9 %all-to-all-start.1 = ((f32[128,32,128]{2,1,0:T(8,128)}), f32[128,32,128]{2,1,0:T(8,128)}, u32[]{:S(2)}, u32[]{:S(2)}) async-start(f32[128,32,128]{2,1,0:T(8,128)} %bitcast.11), calls=%async_computation.1 | async-start | bytes 4194304 | tf_op jit(solution)/shard_map/all_to_all | solution.py:535
  71.2 1.1 slice.3
  72.2 1.2 %collective-permute-start = (f32[128,8,128]{2,1,0:T(8,128)S(1)}, f32[128,8,128]{2,1,0:T(8,128)}, u32[]{:S(2)}, u32[]{:S(2)}) collective-permute-start(f32[128,8,128]{2,1,0:T(8,128)S(1)} %slice.3), channel_id=1, source_target_pairs={{0,8},{8,0},{16,24},{24,16},{32,40},{40,32},{48,56},{56,48},{64,72... | collective-permute-start | bytes 1572872 | tf_op jit(solution)/shard_map/ppermute | solution.py:534
  73.5 17.7 %patch_0.1 = (f32[16,64,128]{2,1,0:T(8,128)}, f32[64,128]{1,0:T(8,128)}, f32[16,128]{1,0:T(8,128)}, f32[16,128]{1,0:T(8,128)}, bf16[256,1280]{1,0:T(8,128)(2,1)}, /*index=5*/bf16[1280,256]{1,0:T(8,128)(2,1)}) custom-call(s32[1]{0:T(128)} %bitcast.odd_ref, f32[128,56,128]{2,1,0:T(8,128)} %all-to-all-done.first_ref, f32[16,128]{1,0:T(8,128)} %start_rows.1.start_ref), custom_call_target="tpu_custom_call" | custom-call | flops 2726297600 | bytes 3276800 | tf_op jit(solution)/shard_map/patch_0/pallas_call | solution.py:509
  91.2 0.0 collective-permute-done.edge_ref
  91.2 9.1 %all-to-all-done.1.second_ref = f32[128,32,128]{2,1,0:T(8,128)} async-done(((f32[128,32,128]{2,1,0:T(8,128)}), f32[128,32,128]{2,1,0:T(8,128)}, u32[]{:S(2)}, u32[]{:S(2)}) %all-to-all-start.1) | async-done | bytes 2097184 | tf_op jit(solution)/shard_map/all_to_all | solution.py:535
  100.3 16.6 %patch_1.1 = (f32[16,64,128]{2,1,0:T(8,128)}, f32[64,128]{1,0:T(8,128)}, f32[2,16,128]{2,1,0:T(8,128)}) custom-call(s32[1]{0:T(128)} %bitcast.odd_ref, f32[128,32,128]{2,1,0:T(8,128)} %all-to-all-done.1.second_ref, f32[128,56,128]{2,1,0:T(8,128)} %all-to-all-done.first_ref, f32[128,8,128]{2,1,0:T(8,128)} %collective-permute-done.edge_ref, ...), custom_call_target="tpu_custom_call" | custom-call | flops 2726297600 | bytes 3276800 | tf_op jit(solution)/shard_map/patch_1/pallas_call | solution.py:509
Async XLA Ops:
  6.8 58.4 %all-to-all-start = ((f32[128,56,128]{2,1,0:T(8,128)}), f32[128,56,128]{2,1,0:T(8,128)}, u32[]{:S(2)}, u32[]{:S(2)}) async-start(f32[128,56,128]{2,1,0:T(8,128)} %bitcast.10), calls=%async_computation | async-start | bytes 7340032 | tf_op jit(solution)/shard_map/all_to_all | solution.py:531
  65.2 35.1 %all-to-all-start.1 = ((f32[128,32,128]{2,1,0:T(8,128)}), f32[128,32,128]{2,1,0:T(8,128)}, u32[]{:S(2)}, u32[]{:S(2)}) async-start(f32[128,32,128]{2,1,0:T(8,128)} %bitcast.11), calls=%async_computation.1 | async-start | bytes 4194304 | tf_op jit(solution)/shard_map/all_to_all | solution.py:535
  72.2 18.9 %collective-permute-start = (f32[128,8,128]{2,1,0:T(8,128)S(1)}, f32[128,8,128]{2,1,0:T(8,128)}, u32[]{:S(2)}, u32[]{:S(2)}) collective-permute-start(f32[128,8,128]{2,1,0:T(8,128)S(1)} %slice.3), channel_id=1, source_target_pairs={{0,8},{8,0},{16,24},{24,16},{32,40},{40,32},{48,56},{56,48},{64,72... | collective-permute-start | bytes 1572872 | tf_op jit(solution)/shard_map/ppermute | solution.py:534

commit v5 on v4

--- a/solution.py
+++ b/solution.py
@@ -18,7 +18,7 @@
 GROUP = 8
 HALF = 64
 SHARED = 16
-FIRST_ROWS = 56
+FIRST_ROWS = 48
 UNROLL = 4
 SECOND_ROWS = 32
 
@@ -62,7 +62,7 @@
     from_here = lane < LANES - turn
     landing = (lane + turn) % LANES
     to_next = landing < 16
-    needed = POSITIONS if exchange == 0 else 8
+    needed = POSITIONS - 1 if exchange == 0 else 8
 
     def rolled(tile, amount):
         return pltpu.roll(tile, (turn + amount) % LANES, 1)
@@ -105,19 +105,23 @@
                 before = following
             else:
                 after = [jnp.where(from_here | (landing >= MARGIN), 0.0, b) for b in before]
-            joined = [jnp.where(to_next, a, h) for a, h in zip(after, here)]
+            joined = [jnp.where(to_next, a, h) for a, h in zip(after, here)] if exchange else None
             if exchange == 0:
                 tile = rolled(here[8], 0)
                 for p in (1, 2, 3):
                     tile = jnp.where(lane >= HALF + SHARED * p, rolled(here[p], SHARED * p), tile)
-                staged[strip, band, 0:8, :] = tile
-                tile = rolled(joined[8], 48)
+                if strip == 0:
+                    begin = tile
+                else:
+                    staged[strip, band, 0:8, :] = tile
+                if strip == strips - 1:
+                    begin = jnp.where(lane < MARGIN, rolled(after[8], 0), begin)
+                    staged[0, band, 0:8, :] = begin
+                tile = rolled(here[8], 48)
+                tile = jnp.where(lane >= HALF - SHARED, rolled(here[0], LANES - SHARED), tile)
                 for p in (4, 5, 6, 7):
                     tile = jnp.where(lane >= SHARED * p, rolled(here[p], SHARED * (p - 4)), tile)
                 staged[strip, band, 8:16, :] = tile
-                tile = jnp.where(lane < HALF + SHARED, rolled(here[9], 0), rolled(here[0], SHARED))
-                tile = jnp.where(lane < HALF + 2 * SHARED, tile, 0.0)
-                staged[strip, band, 48:56, :] = tile
                 source, amounts, base = here, (0, HALF), 2 * GROUP
             else:
                 source, amounts, base = joined, (48, 112), 0
@@ -359,14 +363,14 @@
 NEXT_ROWS = 10
 
 
-def patch_0_kernel(odd_ref, first_ref, start_ref, *refs):
-    spatial_ref, mean_ref, basis_ref, next_means, next_movie_out, next_turned_out = refs[:6]
-    raw, start, movie, turned, next_movie, next_turned = refs[6:12]
-    means, projected, packed, sems = refs[12:]
+def patch_0_kernel(place_ref, first_ref, edge_ref, start_ref, *refs):
+    spatial_ref, mean_ref, basis_ref, next_means, begin_ref = refs[:5]
+    next_movie_out, next_turned_out = refs[5:7]
+    raw, start, movie, turned, next_movie, next_turned = refs[7:13]
+    means, projected, packed, sems = refs[13:]
     frames = first_ref.shape[0]
-    copies = [
-        tile_copy(first_ref, g, raw.at[i], sems.at[i]) for i, g in enumerate((2, 3, 4, 5, 0, 1, 6))
-    ]
+    sources = [(first_ref, g) for g in (2, 3, 4, 5, 0, 1)] + [(edge_ref, 0)]
+    copies = [tile_copy(ref, g, raw.at[i], sems.at[i]) for i, (ref, g) in enumerate(sources)]
     copies.append(pltpu.make_async_copy(start_ref, start, sems.at[7]))
     for copy in copies:
         copy.start()
@@ -378,43 +382,49 @@
     def read(i, s):
         return raw[i, pl.ds(s, frames, stride=GROUP), :]
 
-    for i in range(5):
+    for i in range(4):
         copies[i].wait()
 
         @pl.loop(0, GROUP, unroll=UNROLL)
         def _(s, i=i):
             keep_row(GROUP * i + s, read(i, s), movie, turned, means)
 
-    for copy in copies[5:]:
+    for copy in copies[4:]:
         copy.wait()
-    lower = lane_ids((frames, LANES)) < HALF
+    lane = lane_ids((frames, LANES))
+    lower = lane < HALF
+    inside = lane >= MARGIN * place_ref[1]
 
     @pl.loop(0, GROUP, unroll=2)
     def _(s):
-        edge = read(5, s)
-        keep_row(40 + s, jnp.where(lower, read(6, s), edge), movie, turned, means)
-        both = jnp.where(lower, pltpu.roll(read(4, s), HALF, 1), edge)
+        own, edge = read(4, s), read(5, s)
+        keep_row(32 + s, jnp.where(inside, own, 0.0), movie, turned, means)
+        both = jnp.where(inside, jnp.where(lower, read(6, s), edge), 0.0)
+        keep_row(40 + s, both, movie, turned, means)
+        both = jnp.where(lower, pltpu.roll(own, HALF, 1), edge)
         keep_row(s, both, next_movie, next_turned, next_means)
 
-    once = (odd_ref[0] >= 0).astype(jnp.int32)
-    for row in range(2):
-        values = narrow_rows(raw.at[6], HALF + SHARED * row)
+    once = (place_ref[0] >= 0).astype(jnp.int32)
+    for row, (tile, lane0) in enumerate(((6, HALF), (5, HALF - SHARED))):
+        begin_ref[frames * row : frames * row + frames, :] = narrow_rows(raw.at[4 + 2 * row], 0)
+        values = narrow_rows(raw.at[tile], lane0)
         keep_row(48 + row, values, movie, turned, means)
         keep_row(GROUP + row, values, next_movie, next_turned, next_means)
     for copy in results:
         copy.start()
     basis, level = iterate(start[...], movie, turned, projected, frames, once)
     outs = (spatial_ref, mean_ref, basis_ref)
-    finish(0, odd_ref[0], basis, level, means, projected, packed, outs, None)
+    finish(0, place_ref[0], basis, level, means, projected, packed, outs, None)
     for copy in results:
         copy.wait()
 
 
 def patch_1_kernel(
-    odd_ref,
+    place_ref,
     second_ref,
     first_ref,
     edge_ref,
+    begin_ref,
     next_movie_in,
     next_turned_in,
     next_means_in,
@@ -422,17 +432,17 @@
     *refs,
 ):
     earlier_in, outs = refs[:3], refs[3:6]
-    raw, start, next_means = refs[6:9]
-    earlier = refs[9:12]
-    movie, turned, means, projected, packed, sems = refs[12:]
+    raw, begin, start, next_means = refs[6:10]
+    earlier = refs[10:13]
+    movie, turned, means, projected, packed, sems = refs[13:]
     done = PIXEL_ROWS - NEXT_ROWS
     own = done * LANES
     frames = second_ref.shape[0]
     tiles = SECOND_ROWS // GROUP
-    sources = [(second_ref, i) for i in range(tiles)] + [(first_ref, 1), (edge_ref, 0)]
+    sources = [(second_ref, i) for i in range(tiles)] + [(first_ref, 1), (edge_ref, 1)]
     copies = [tile_copy(ref, g, raw.at[i], sems.at[i]) for i, (ref, g) in enumerate(sources)]
-    sources = (next_movie_in, next_turned_in, next_means_in, start_ref, *earlier_in)
-    targets = (movie.at[:, own:], turned.at[own:, :], next_means, start, *earlier)
+    sources = (begin_ref, next_movie_in, next_turned_in, next_means_in, start_ref, *earlier_in)
+    targets = (begin, movie.at[:, own:], turned.at[own:, :], next_means, start, *earlier)
     for source, target in zip(sources, targets):
         copies.append(pltpu.make_async_copy(source, target, sems.at[len(copies)]))
     for copy in copies:
@@ -450,17 +460,26 @@
 
     for copy in copies[tiles:]:
         copy.wait()
-    lower = lane_ids((frames, LANES)) < HALF
+    lane = lane_ids((frames, LANES))
+    lower = lane < HALF
+    late = lane % HALF >= HALF - SHARED
+    outside = lane % SHARED >= SHARED - MARGIN * place_ref[2]
 
     @pl.loop(0, GROUP, unroll=UNROLL)
     def _(s):
         both = jnp.where(lower, read(tiles, s), pltpu.roll(read(tiles + 1, s), HALF, 1))
+        ends = [jnp.where(outside, 0.0, begin[frames * i : frames * i + frames, :]) for i in (0, 1)]
+        ends = [
+            pltpu.roll(end, (spot - SHARED * s + LANES) % LANES, 1)
+            for end, spot in zip(ends, (HALF - SHARED, LANES - SHARED))
+        ]
+        both = jnp.where(late, jnp.where(lower, ends[0], ends[1]), both)
         keep_row(SECOND_ROWS + s, both, movie, turned, means)
 
-    once = (odd_ref[0] >= 0).astype(jnp.int32)
+    once = (place_ref[0] >= 0).astype(jnp.int32)
     means[done : done + GROUP, :] = next_means[0:GROUP, :]
     basis, level = iterate(start[...], movie, turned, projected, frames, once)
-    finish(1, odd_ref[0], basis, level, means, projected, packed, outs, earlier)
+    finish(1, place_ref[0], basis, level, means, projected, packed, outs, earlier)
 
 
 def decompose(patch, *operands):
@@ -484,8 +503,9 @@
     next_means = (16, LANES)
     if patch == 0:
         shapes.append(jax.ShapeDtypeStruct(next_means, jnp.float32))
+        shapes.append(jax.ShapeDtypeStruct((2 * frames, LANES), jnp.float32))
         shapes += parts(NEXT_ROWS, jax.ShapeDtypeStruct)
-        out_specs += [vmem, hbm, hbm]
+        out_specs += [vmem, vmem, hbm, hbm]
         scratch = [
             pltpu.VMEM((7, frames * GROUP, LANES), jnp.float32),
             start,
@@ -495,6 +515,7 @@
     else:
         scratch = [
             pltpu.VMEM((6, frames * GROUP, LANES), jnp.float32),
+            pltpu.VMEM((2 * frames, LANES), jnp.float32),
             start,
             pltpu.VMEM(next_means, jnp.float32),
             *(pltpu.VMEM(value.shape, jnp.float32) for value in operands[-3:]),
@@ -504,7 +525,7 @@
         pltpu.VMEM((56, LANES), jnp.float32),
         pltpu.VMEM((RANK, PIXEL_ROWS * LANES), jnp.float32),
         pltpu.VMEM((RANK * 48, LANES), jnp.float32),
-        pltpu.SemaphoreType.DMA((13,)),
+        pltpu.SemaphoreType.DMA((14,)),
     ]
     return pl.pallas_call(
         patch_1_kernel if patch else patch_0_kernel,
@@ -525,17 +546,20 @@
 def on_device(frames, shifts, start_basis):
     n_rows = lax.axis_size("py")
     n_cols = lax.axis_size("px")
-    odd = (lax.axis_index("py") & 1).astype(jnp.int32).reshape(1)
+    column = lax.axis_index("px")
+    place = [lax.axis_index("py") & 1, column == 0, column == n_cols - 1]
+    place = jnp.stack([value.astype(jnp.int32) for value in place])
     first = spread(0, frames[0], shifts, n_rows, n_cols)
     second = spread(1, frames[0], shifts, n_rows, n_cols)
     first = lax.all_to_all(first, ("px", "py"), split_axis=0, concat_axis=0, tiled=True)
     first, start, second = lax.optimization_barrier((first, start_rows(start_basis.T), second))
     pairs = [(i, i ^ 1) for i in range(n_rows)]
-    edge = lax.ppermute(first[:, GROUP : 2 * GROUP], "py", pairs)
+    edge = lax.ppermute(first[:, : 2 * GROUP], "py", pairs)
     second = lax.all_to_all(second, ("px", "py"), split_axis=0, concat_axis=0, tiled=True)
-    *left, next_means, next_movie, next_turned = decompose(0, odd, first, start)
+    *left, next_means, begin, next_movie, next_turned = decompose(0, place, first, edge, start)
+    begin = lax.ppermute(begin, "px", [(i, (i - 1) % n_cols) for i in range(n_cols)])
     spatial, background, bases = decompose(
-        1, odd, second, first, edge, next_movie, next_turned, next_means, start, *left
+        1, place, second, first, edge, begin, next_movie, next_turned, next_means, start, *left
     )
     return (spatial, bases.swapaxes(1, 2)[None], background)
 

time: 117 us -> 114 us (0.974)
  waiting for transfers between devices: 49.3 us -> 39.5 us
  starting transfers between devices: 19.1 us -> 22 us
  Pallas kernels: 46.8 us -> 48.8 us
    all_to_all x1, waiting for transfers between devices: 9.12 us -> 0.01 us  [on_device(): lax.all_to_all(second, ('px', 'py'), split_axis=0, concat_axis=0, tiled=T...]
    all_to_all x1, waiting for transfers between devices: 40.2 us -> 34.3 us  [on_device(): lax.all_to_all(first, ('px', 'py'), split_axis=0, concat_axis=0, tiled=True)]
    ppermute x1 -> x2, waiting for transfers between devices: 0.01 us -> 5.19 us  [the longest x1 3.36 us: on_device(): lax.ppermute(begin, 'px', [(i, (i - 1) % n_cols) for i in range(n_cols)])]
    ppermute x1 -> x2, starting transfers between devices: 1.22 us -> 4.19 us  [the longest x1 2.97 us: on_device(): lax.ppermute(begin, 'px', [(i, (i - 1) % n_cols) for i in range(n_cols)])]
    pallas_call x2, Pallas kernels: 34.3 us -> 36.4 us  [decompose(): pl.pallas_call(patch_1_kernel if patch else patch_0_kernel, out_shape=tup...]
  transfers between devices with their start and end apart: 3 -> 4, of which waited for: 2 -> 3; matrix products, arithmetic and copies ran while one was open for 1% -> 2% of each run, Pallas kernels for 21% -> 22%
where the time goes in v5:
time: 114 us
  Pallas kernels  48.8 us (43%)
  waiting for transfers between devices  39.5 us (35%)
  starting transfers between devices  22 us (19%)
  local copies, waits for them, and re-layouts  1.96 us (2%)
    pallas_call x2, Pallas kernels, decompose(): pl.pallas_call(patch_1_kernel if patch else patch_0_kernel, out_shape=tup...  36.4 us
    all_to_all x1, waiting for transfers between devices, on_device(): lax.all_to_all(first, ('px', 'py'), split_axis=0, concat_axis=0, tiled=True)  34.3 us
    all_to_all x1, starting transfers between devices, on_device(): lax.all_to_all(first, ('px', 'py'), split_axis=0, concat_axis=0, tiled=True)  11.9 us
    pallas_call x2, Pallas kernels, spread(): pl.pallas_call(lambda *refs: spread_kernel(exchange, *refs), out_shape=ja...  10.6 us
    all_to_all x1, starting transfers between devices, on_device(): lax.all_to_all(second, ('px', 'py'), split_axis=0, concat_axis=0, tiled=T...  5.93 us
    ppermute x1, waiting for transfers between devices, on_device(): lax.ppermute(begin, 'px', [(i, (i - 1) % n_cols) for i in range(n_cols)])  3.36 us
    ppermute x1, starting transfers between devices, on_device(): lax.ppermute(begin, 'px', [(i, (i - 1) % n_cols) for i in range(n_cols)])  2.97 us
  transfers between devices with their start and end apart: 4, of which 3 were waited for; matrix products, arithmetic and copies ran while one was open for 2% of the time, Pallas kernels for 22%

profile of v5, /device:TPU:1, one launch (start us, length us, event | category | flops | bytes accessed | tf_op | source)
XLA Modules:
  0.0 113.5 jit_solution(6812706438747223628)
XLA Ops:
  0.6 6.1 %spread_0.1 = f32[8,16,48,128]{3,2,1,0:T(8,128)} custom-call(s32[1,2]{1,0:T(1,128)} %refs_0_.3, f32[1024,1024]{1,0:T(8,128)} %bitcast.10), custom_call_target="tpu_custom_call" | custom-call | tf_op jit(solution)/shard_map/spread_0/pallas_call | solution.py:144
  6.7 11.9 %all-to-all-start = ((f32[128,48,128]{2,1,0:T(8,128)}), f32[128,48,128]{2,1,0:T(8,128)}, u32[]{:S(2)}, u32[]{:S(2)}) async-start(f32[128,48,128]{2,1,0:T(8,128)} %bitcast.12), calls=%async_computation | async-start | bytes 6291456 | tf_op jit(solution)/shard_map/all_to_all | solution.py:554
  18.6 4.5 %spread_1.1 = f32[8,16,32,128]{3,2,1,0:T(8,128)} custom-call(s32[1,2]{1,0:T(1,128)} %refs_0_.3, f32[1024,1024]{1,0:T(8,128)} %bitcast.11), custom_call_target="tpu_custom_call" | custom-call | tf_op jit(solution)/shard_map/spread_1/pallas_call | solution.py:144
  23.1 1.8 %start_rows.1.start_ref = f32[16,128]{1,0:T(8,128)} custom-call(f32[16,128]{1,0:T(8,128)} %bitcast.14), custom_call_target="tpu_custom_call" | custom-call | tf_op jit(solution)/shard_map/start_rows/pallas_call | solution.py:242
  24.9 34.3 %all-to-all-done.first_ref = f32[128,48,128]{2,1,0:T(8,128)} async-done(((f32[128,48,128]{2,1,0:T(8,128)}), f32[128,48,128]{2,1,0:T(8,128)}, u32[]{:S(2)}, u32[]{:S(2)}) %all-to-all-start) | async-done | bytes 3145760 | tf_op jit(solution)/shard_map/all_to_all | solution.py:554
  59.2 5.9 %all-to-all-start.1 = ((f32[128,32,128]{2,1,0:T(8,128)}), f32[128,32,128]{2,1,0:T(8,128)}, u32[]{:S(2)}, u32[]{:S(2)}) async-start(f32[128,32,128]{2,1,0:T(8,128)} %bitcast.13), calls=%async_computation.1 | async-start | bytes 4194304 | tf_op jit(solution)/shard_map/all_to_all | solution.py:558
  65.2 1.3 %slice.3 = f32[128,16,128]{2,1,0:T(8,128)S(1)} slice(f32[128,48,128]{2,1,0:T(8,128)} %all-to-all-done.first_ref), slice={[0:128], [0:16], [0:128]} | slice | bytes 2097152 | tf_op jit(solution)/shard_map/slice | solution.py:557
  66.5 1.2 %collective-permute-start = (f32[128,16,128]{2,1,0:T(8,128)S(1)}, f32[128,16,128]{2,1,0:T(8,128)}, u32[]{:S(2)}, u32[]{:S(2)}) collective-permute-start(f32[128,16,128]{2,1,0:T(8,128)S(1)} %slice.3), channel_id=1, source_target_pairs={{0,8},{8,0},{16,24},{24,16},{32,40},{40,32},{48,56},{56,48},{64,72... | collective-permute-start | bytes 3145736 | tf_op jit(solution)/shard_map/ppermute | solution.py:557
  67.7 0.6 pad_add_fusion.place_ref
  68.3 1.8 %collective-permute-done.edge_ref = f32[128,16,128]{2,1,0:T(8,128)} collective-permute-done((f32[128,16,128]{2,1,0:T(8,128)S(1)}, f32[128,16,128]{2,1,0:T(8,128)}, u32[]{:S(2)}, u32[]{:S(2)}) %collective-permute-start) | collective-permute-done | bytes 1048608 | tf_op jit(solution)/shard_map/ppermute | solution.py:557
  70.1 18.7 %patch_0.1 = (f32[16,64,128]{2,1,0:T(8,128)}, f32[64,128]{1,0:T(8,128)}, f32[16,128]{1,0:T(8,128)}, f32[16,128]{1,0:T(8,128)}, f32[256,128]{1,0:T(8,128)}, /*ind...) custom-call(s32[3]{0:T(128)} %pad_add_fusion.place_ref, f32[128,48,128]{2,1,0:T(8,128)} %all-to-all-done.first_ref, ...), custom_call_target="tpu_custom_call" | custom-call | flops 2726297600 | bytes 3276800 | tf_op jit(solution)/shard_map/patch_0/pallas_call | solution.py:530
  88.8 3.0 %collective-permute-start.1 = (f32[256,128]{1,0:T(8,128)}, f32[256,128]{1,0:T(8,128)S(1)}, u32[]{:S(2)}, u32[]{:S(2)}) collective-permute-start(f32[256,128]{1,0:T(8,128)} %get-tuple-element.19), channel_id=1, source_target_pairs={{0,7},{1,0},{2,1},{3,2},{4,3},{5,4},{6,5},{7,6},{8,15},{9,8},{10,9... | collective-permute-start | bytes 393224 | tf_op jit(solution)/shard_map/ppermute | solution.py:560
  91.8 3.4 %collective-permute-done.1.begin_ref = f32[256,128]{1,0:T(8,128)S(1)} collective-permute-done((f32[256,128]{1,0:T(8,128)}, f32[256,128]{1,0:T(8,128)S(1)}, u32[]{:S(2)}, u32[]{:S(2)}) %collective-permute-start.1) | collective-permute-done | bytes 131104 | tf_op jit(solution)/shard_map/ppermute | solution.py:560
  95.1 0.0 copy-start
  95.1 0.0 all-to-all-done.1.second_ref
  95.2 0.6 copy-done
  95.8 17.7 %patch_1.1 = (f32[16,64,128]{2,1,0:T(8,128)}, f32[64,128]{1,0:T(8,128)}, f32[2,16,128]{2,1,0:T(8,128)}) custom-call(s32[3]{0:T(128)} %pad_add_fusion.place_ref, f32[128,32,128]{2,1,0:T(8,128)} %all-to-all-done.1.second_ref, f32[128,48,128]{2,1,0:T(8,128)} %all-to-all-done.first_ref, f32[128,16,128]{2,1,0:T(8,128)} %collective-permute-done.edge_ref, ...), custom_call_target="tpu_custom_call" | custom-call | flops 2726297600 | bytes 3276800 | tf_op jit(solution)/shard_map/patch_1/pallas_call | solution.py:530
Async XLA Ops:
  6.7 52.5 %all-to-all-start = ((f32[128,48,128]{2,1,0:T(8,128)}), f32[128,48,128]{2,1,0:T(8,128)}, u32[]{:S(2)}, u32[]{:S(2)}) async-start(f32[128,48,128]{2,1,0:T(8,128)} %bitcast.12), calls=%async_computation | async-start | bytes 6291456 | tf_op jit(solution)/shard_map/all_to_all | solution.py:554
  59.2 35.9 %all-to-all-start.1 = ((f32[128,32,128]{2,1,0:T(8,128)}), f32[128,32,128]{2,1,0:T(8,128)}, u32[]{:S(2)}, u32[]{:S(2)}) async-start(f32[128,32,128]{2,1,0:T(8,128)} %bitcast.13), calls=%async_computation.1 | async-start | bytes 4194304 | tf_op jit(solution)/shard_map/all_to_all | solution.py:558
  66.5 3.6 %collective-permute-start = (f32[128,16,128]{2,1,0:T(8,128)S(1)}, f32[128,16,128]{2,1,0:T(8,128)}, u32[]{:S(2)}, u32[]{:S(2)}) collective-permute-start(f32[128,16,128]{2,1,0:T(8,128)S(1)} %slice.3), channel_id=1, source_target_pairs={{0,8},{8,0},{16,24},{24,16},{32,40},{40,32},{48,56},{56,48},{64,72... | collective-permute-start | bytes 3145736 | tf_op jit(solution)/shard_map/ppermute | solution.py:557
  88.8 6.3 %collective-permute-start.1 = (f32[256,128]{1,0:T(8,128)}, f32[256,128]{1,0:T(8,128)S(1)}, u32[]{:S(2)}, u32[]{:S(2)}) collective-permute-start(f32[256,128]{1,0:T(8,128)} %get-tuple-element.19), channel_id=1, source_target_pairs={{0,7},{1,0},{2,1},{3,2},{4,3},{5,4},{6,5},{7,6},{8,15},{9,8},{10,9... | collective-permute-start | bytes 393224 | tf_op jit(solution)/shard_map/ppermute | solution.py:560
  95.1 0.7 copy-start

commit v6 on v5

--- a/solution.py
+++ b/solution.py
@@ -394,6 +394,7 @@
     lane = lane_ids((frames, LANES))
     lower = lane < HALF
     inside = lane >= MARGIN * place_ref[1]
+    unsent = lane % SHARED >= SHARED - MARGIN * place_ref[1]
 
     @pl.loop(0, GROUP, unroll=2)
     def _(s):
@@ -406,7 +407,12 @@
 
     once = (place_ref[0] >= 0).astype(jnp.int32)
     for row, (tile, lane0) in enumerate(((6, HALF), (5, HALF - SHARED))):
-        begin_ref[frames * row : frames * row + frames, :] = narrow_rows(raw.at[4 + 2 * row], 0)
+        ends = jnp.zeros((frames, LANES), jnp.float32)
+        for k in range(4):
+            for side, values in ((0, read(4, 4 * row + k)), (4, read(6, 4 * row + k))):
+                values = pltpu.roll(values, SHARED * (side + k), 1) if side + k else values
+                ends = jnp.where(lane // SHARED == side + k, values, ends)
+        begin_ref[frames * row : frames * row + frames, :] = jnp.where(unsent, 0.0, ends)
         values = narrow_rows(raw.at[tile], lane0)
         keep_row(48 + row, values, movie, turned, means)
         keep_row(GROUP + row, values, next_movie, next_turned, next_means)
@@ -463,17 +469,13 @@
     lane = lane_ids((frames, LANES))
     lower = lane < HALF
     late = lane % HALF >= HALF - SHARED
-    outside = lane % SHARED >= SHARED - MARGIN * place_ref[2]
 
     @pl.loop(0, GROUP, unroll=UNROLL)
     def _(s):
         both = jnp.where(lower, read(tiles, s), pltpu.roll(read(tiles + 1, s), HALF, 1))
-        ends = [jnp.where(outside, 0.0, begin[frames * i : frames * i + frames, :]) for i in (0, 1)]
-        ends = [
-            pltpu.roll(end, (spot - SHARED * s + LANES) % LANES, 1)
-            for end, spot in zip(ends, (HALF - SHARED, LANES - SHARED))
-        ]
-        both = jnp.where(late, jnp.where(lower, ends[0], ends[1]), both)
+        ends = begin[pl.ds(pl.multiple_of(s // 4 * frames, frames), frames), :]
+        ends = pltpu.roll(ends, (HALF - SHARED - SHARED * (s % 4)) % LANES, 1)
+        both = jnp.where(late, ends, both)
         keep_row(SECOND_ROWS + s, both, movie, turned, means)
 
     once = (place_ref[0] >= 0).astype(jnp.int32)
@@ -547,12 +549,14 @@
     n_rows = lax.axis_size("py")
     n_cols = lax.axis_size("px")
     column = lax.axis_index("px")
-    place = [lax.axis_index("py") & 1, column == 0, column == n_cols - 1]
+    place = [lax.axis_index("py") & 1, column == 0]
     place = jnp.stack([value.astype(jnp.int32) for value in place])
     first = spread(0, frames[0], shifts, n_rows, n_cols)
     second = spread(1, frames[0], shifts, n_rows, n_cols)
     first = lax.all_to_all(first, ("px", "py"), split_axis=0, concat_axis=0, tiled=True)
-    first, start, second = lax.optimization_barrier((first, start_rows(start_basis.T), second))
+    first, start, second, place = lax.optimization_barrier(
+        (first, start_rows(start_basis.T), second, place)
+    )
     pairs = [(i, i ^ 1) for i in range(n_rows)]
     edge = lax.ppermute(first[:, : 2 * GROUP], "py", pairs)
     second = lax.all_to_all(second, ("px", "py"), split_axis=0, concat_axis=0, tiled=True)

time: 114 us -> 114 us (level)
  no operation moved by 1% of the time
where the time goes in v6:
time: 114 us; the launch traced here: 113 us
  Pallas kernels  48.6 us (43%)
  waiting for transfers between devices  39.5 us (35%)
  starting transfers between devices  22 us (19%)
  local copies, waits for them, and re-layouts  1.96 us (2%)
    pallas_call x2, Pallas kernels, decompose(): pl.pallas_call(patch_1_kernel if patch else patch_0_kernel, out_shape=tup...  36.2 us
    all_to_all x1, waiting for transfers between devices, on_device(): lax.all_to_all(first, ('px', 'py'), split_axis=0, concat_axis=0, tiled=True)  33.7 us
    all_to_all x1, starting transfers between devices, on_device(): lax.all_to_all(first, ('px', 'py'), split_axis=0, concat_axis=0, tiled=True)  11.9 us
    pallas_call x2, Pallas kernels, spread(): pl.pallas_call(lambda *refs: spread_kernel(exchange, *refs), out_shape=ja...  10.6 us
    all_to_all x1, starting transfers between devices, on_device(): lax.all_to_all(second, ('px', 'py'), split_axis=0, concat_axis=0, tiled=T...  5.93 us
    ppermute x1, waiting for transfers between devices, on_device(): lax.ppermute(begin, 'px', [(i, (i - 1) % n_cols) for i in range(n_cols)])  3.36 us
    ppermute x1, starting transfers between devices, on_device(): lax.ppermute(begin, 'px', [(i, (i - 1) % n_cols) for i in range(n_cols)])  2.97 us
    ppermute x1, waiting for transfers between devices, on_device(): edge = lax.ppermute(first[:, :2 * GROUP], 'py', pairs)  2.42 us
  transfers between devices with their start and end apart: 4, of which 3 were waited for; matrix products, arithmetic and copies ran while one was open for 2% of the time, Pallas kernels for 22%

profile of v6, /device:TPU:1, one launch (start us, length us, event | category | flops | bytes accessed | tf_op | source)
XLA Modules:
  0.0 113.4 jit_solution(10426911165443701030)
XLA Ops:
  0.6 6.1 %spread_0.1 = f32[8,16,48,128]{3,2,1,0:T(8,128)} custom-call(s32[1,2]{1,0:T(1,128)} %refs_0_.3, f32[1024,1024]{1,0:T(8,128)} %bitcast.9), custom_call_target="tpu_custom_call" | custom-call | tf_op jit(solution)/shard_map/spread_0/pallas_call | solution.py:144
  6.7 11.9 %all-to-all-start = ((f32[128,48,128]{2,1,0:T(8,128)}), f32[128,48,128]{2,1,0:T(8,128)}, u32[]{:S(2)}, u32[]{:S(2)}) async-start(f32[128,48,128]{2,1,0:T(8,128)} %bitcast.11), calls=%async_computation | async-start | bytes 6291456 | tf_op jit(solution)/shard_map/all_to_all | solution.py:556
  18.6 4.5 %spread_1.1 = f32[8,16,32,128]{3,2,1,0:T(8,128)} custom-call(s32[1,2]{1,0:T(1,128)} %refs_0_.3, f32[1024,1024]{1,0:T(8,128)} %bitcast.10), custom_call_target="tpu_custom_call" | custom-call | tf_op jit(solution)/shard_map/spread_1/pallas_call | solution.py:144
  23.1 1.8 %start_rows.1.start_ref = f32[16,128]{1,0:T(8,128)} custom-call(f32[16,128]{1,0:T(8,128)} %bitcast.13), custom_call_target="tpu_custom_call" | custom-call | tf_op jit(solution)/shard_map/start_rows/pallas_call | solution.py:242
  24.9 0.6 pad_add_fusion.place_ref
  25.5 33.7 %all-to-all-done.first_ref = f32[128,48,128]{2,1,0:T(8,128)} async-done(((f32[128,48,128]{2,1,0:T(8,128)}), f32[128,48,128]{2,1,0:T(8,128)}, u32[]{:S(2)}, u32[]{:S(2)}) %all-to-all-start) | async-done | bytes 3145760 | tf_op jit(solution)/shard_map/all_to_all | solution.py:556
  59.2 5.9 %all-to-all-start.1 = ((f32[128,32,128]{2,1,0:T(8,128)}), f32[128,32,128]{2,1,0:T(8,128)}, u32[]{:S(2)}, u32[]{:S(2)}) async-start(f32[128,32,128]{2,1,0:T(8,128)} %bitcast.12), calls=%async_computation.1 | async-start | bytes 4194304 | tf_op jit(solution)/shard_map/all_to_all | solution.py:562
  65.2 1.3 %slice.3 = f32[128,16,128]{2,1,0:T(8,128)S(1)} slice(f32[128,48,128]{2,1,0:T(8,128)} %all-to-all-done.first_ref), slice={[0:128], [0:16], [0:128]} | slice | bytes 2097152 | tf_op jit(solution)/shard_map/slice | solution.py:561
  66.5 1.2 %collective-permute-start = (f32[128,16,128]{2,1,0:T(8,128)S(1)}, f32[128,16,128]{2,1,0:T(8,128)}, u32[]{:S(2)}, u32[]{:S(2)}) collective-permute-start(f32[128,16,128]{2,1,0:T(8,128)S(1)} %slice.3), channel_id=1, source_target_pairs={{0,8},{8,0},{16,24},{24,16},{32,40},{40,32},{48,56},{56,48},{64,72... | collective-permute-start | bytes 3145736 | tf_op jit(solution)/shard_map/ppermute | solution.py:561
  67.7 2.4 %collective-permute-done.edge_ref = f32[128,16,128]{2,1,0:T(8,128)} collective-permute-done((f32[128,16,128]{2,1,0:T(8,128)S(1)}, f32[128,16,128]{2,1,0:T(8,128)}, u32[]{:S(2)}, u32[]{:S(2)}) %collective-permute-start) | collective-permute-done | bytes 1048608 | tf_op jit(solution)/shard_map/ppermute | solution.py:561
  70.1 18.7 %patch_0.1 = (f32[16,64,128]{2,1,0:T(8,128)}, f32[64,128]{1,0:T(8,128)}, f32[16,128]{1,0:T(8,128)}, f32[16,128]{1,0:T(8,128)}, f32[256,128]{1,0:T(8,128)}, /*ind...) custom-call(s32[2]{0:T(128)} %pad_add_fusion.place_ref, f32[128,48,128]{2,1,0:T(8,128)} %all-to-all-done.first_ref, ...), custom_call_target="tpu_custom_call" | custom-call | flops 2726297600 | bytes 3276800 | tf_op jit(solution)/shard_map/patch_0/pallas_call | solution.py:532
  88.9 3.0 %collective-permute-start.1 = (f32[256,128]{1,0:T(8,128)}, f32[256,128]{1,0:T(8,128)S(1)}, u32[]{:S(2)}, u32[]{:S(2)}) collective-permute-start(f32[256,128]{1,0:T(8,128)} %get-tuple-element.21), channel_id=1, source_target_pairs={{0,7},{1,0},{2,1},{3,2},{4,3},{5,4},{6,5},{7,6},{8,15},{9,8},{10,9... | collective-permute-start | bytes 393224 | tf_op jit(solution)/shard_map/ppermute | solution.py:564
  91.8 3.4 %collective-permute-done.1.begin_ref = f32[256,128]{1,0:T(8,128)S(1)} collective-permute-done((f32[256,128]{1,0:T(8,128)}, f32[256,128]{1,0:T(8,128)S(1)}, u32[]{:S(2)}, u32[]{:S(2)}) %collective-permute-start.1) | collective-permute-done | bytes 131104 | tf_op jit(solution)/shard_map/ppermute | solution.py:564
  95.2 0.0 copy-start
  95.2 0.0 all-to-all-done.1.second_ref
  95.2 0.6 copy-done
  95.8 17.5 %patch_1.1 = (f32[16,64,128]{2,1,0:T(8,128)}, f32[64,128]{1,0:T(8,128)}, f32[2,16,128]{2,1,0:T(8,128)}) custom-call(s32[2]{0:T(128)} %pad_add_fusion.place_ref, f32[128,32,128]{2,1,0:T(8,128)} %all-to-all-done.1.second_ref, f32[128,48,128]{2,1,0:T(8,128)} %all-to-all-done.first_ref, f32[128,16,128]{2,1,0:T(8,128)} %collective-permute-done.edge_ref, ...), custom_call_target="tpu_custom_call" | custom-call | flops 2726297600 | bytes 3276800 | tf_op jit(solution)/shard_map/patch_1/pallas_call | solution.py:532
Async XLA Ops:
  6.7 52.5 %all-to-all-start = ((f32[128,48,128]{2,1,0:T(8,128)}), f32[128,48,128]{2,1,0:T(8,128)}, u32[]{:S(2)}, u32[]{:S(2)}) async-start(f32[128,48,128]{2,1,0:T(8,128)} %bitcast.11), calls=%async_computation | async-start | bytes 6291456 | tf_op jit(solution)/shard_map/all_to_all | solution.py:556
  59.2 36.0 %all-to-all-start.1 = ((f32[128,32,128]{2,1,0:T(8,128)}), f32[128,32,128]{2,1,0:T(8,128)}, u32[]{:S(2)}, u32[]{:S(2)}) async-start(f32[128,32,128]{2,1,0:T(8,128)} %bitcast.12), calls=%async_computation.1 | async-start | bytes 4194304 | tf_op jit(solution)/shard_map/all_to_all | solution.py:562
  66.5 3.6 %collective-permute-start = (f32[128,16,128]{2,1,0:T(8,128)S(1)}, f32[128,16,128]{2,1,0:T(8,128)}, u32[]{:S(2)}, u32[]{:S(2)}) collective-permute-start(f32[128,16,128]{2,1,0:T(8,128)S(1)} %slice.3), channel_id=1, source_target_pairs={{0,8},{8,0},{16,24},{24,16},{32,40},{40,32},{48,56},{56,48},{64,72... | collective-permute-start | bytes 3145736 | tf_op jit(solution)/shard_map/ppermute | solution.py:561
  88.9 6.3 %collective-permute-start.1 = (f32[256,128]{1,0:T(8,128)}, f32[256,128]{1,0:T(8,128)S(1)}, u32[]{:S(2)}, u32[]{:S(2)}) collective-permute-start(f32[256,128]{1,0:T(8,128)} %get-tuple-element.21), channel_id=1, source_target_pairs={{0,7},{1,0},{2,1},{3,2},{4,3},{5,4},{6,5},{7,6},{8,15},{9,8},{10,9... | collective-permute-start | bytes 393224 | tf_op jit(solution)/shard_map/ppermute | solution.py:564
  95.2 0.7 copy-start

commit v7 on v6

--- a/solution.py
+++ b/solution.py
@@ -318,8 +318,8 @@
         place(p, jnp.where(from_own, own, both))
 
 
-def finish(patch, odd, basis, level, means, projected, packed, outs, earlier):
-    spatial_ref, mean_ref, basis_ref = outs
+def finish(patch, odd, level, means, projected, packed, outs, earlier):
+    spatial_ref, mean_ref = outs
     tiles = 6
     rows = tiles * GROUP
     keep = lane_ids((GROUP, LANES)) < HALF
@@ -351,12 +351,32 @@
             patch,
             place,
         )
-    scaled = basis * jnp.sqrt(jnp.float32(basis.shape[1]))
-    if patch == 0:
-        basis_ref[...] = scaled
-    else:
-        basis_ref[0] = earlier[2][...]
-        basis_ref[1] = scaled
+
+
+def scaled(basis):
+    return basis * jnp.sqrt(jnp.float32(basis.shape[1]))
+
+
+def finish_0_kernel(place_ref, projected, level, means, spatial_ref, mean_ref, packed):
+    outs = (spatial_ref, mean_ref)
+    finish(0, place_ref[0], level[...], means, projected, packed, outs, None)
+
+
+def finish_0(*operands):
+    vmem = pl.BlockSpec(memory_space=pltpu.VMEM)
+    return pl.pallas_call(
+        finish_0_kernel,
+        out_shape=(
+            jax.ShapeDtypeStruct((RANK, PATCH, LANES), jnp.float32),
+            jax.ShapeDtypeStruct((PATCH, LANES), jnp.float32),
+        ),
+        in_specs=[pl.BlockSpec(memory_space=pltpu.SMEM)] + [vmem] * 3,
+        out_specs=(vmem, vmem),
+        scratch_shapes=[pltpu.VMEM((RANK * 48, LANES), jnp.float32)],
+        compiler_params=pltpu.CompilerParams(vmem_limit_bytes=63 << 20),
+        cost_estimate=pl.CostEstimate(flops=1 << 24, bytes_accessed=1 << 21, transcendentals=0),
+        name="finish_0",
+    )(*operands)
 
 
 PIXEL_ROWS = EDGE * EDGE // LANES
@@ -364,10 +384,9 @@
 
 
 def patch_0_kernel(place_ref, first_ref, edge_ref, start_ref, *refs):
-    spatial_ref, mean_ref, basis_ref, next_means, begin_ref = refs[:5]
-    next_movie_out, next_turned_out = refs[5:7]
-    raw, start, movie, turned, next_movie, next_turned = refs[7:13]
-    means, projected, packed, sems = refs[13:]
+    projected, level_ref, means, basis_ref, next_means, begin_ref = refs[:6]
+    next_movie_out, next_turned_out = refs[6:8]
+    raw, start, movie, turned, next_movie, next_turned, sems = refs[8:]
     frames = first_ref.shape[0]
     sources = [(first_ref, g) for g in (2, 3, 4, 5, 0, 1)] + [(edge_ref, 0)]
     copies = [tile_copy(ref, g, raw.at[i], sems.at[i]) for i, (ref, g) in enumerate(sources)]
@@ -419,8 +438,8 @@
     for copy in results:
         copy.start()
     basis, level = iterate(start[...], movie, turned, projected, frames, once)
-    outs = (spatial_ref, mean_ref, basis_ref)
-    finish(0, place_ref[0], basis, level, means, projected, packed, outs, None)
+    level_ref[...] = jnp.broadcast_to(level, level_ref.shape)
+    basis_ref[...] = scaled(basis)
     for copy in results:
         copy.wait()
 
@@ -481,7 +500,9 @@
     once = (place_ref[0] >= 0).astype(jnp.int32)
     means[done : done + GROUP, :] = next_means[0:GROUP, :]
     basis, level = iterate(start[...], movie, turned, projected, frames, once)
-    finish(1, place_ref[0], basis, level, means, projected, packed, outs, earlier)
+    finish(1, place_ref[0], level, means, projected, packed, outs[:2], earlier)
+    outs[2][0] = earlier[2][...]
+    outs[2][1] = scaled(basis)
 
 
 def decompose(patch, *operands):
@@ -494,13 +515,12 @@
             make((rows * LANES, 2 * frames), jnp.bfloat16),
         ]
 
-    bases = (RANK, frames) if patch == 0 else (2, RANK, frames)
-    shapes = [
-        jax.ShapeDtypeStruct((RANK, PATCH, LANES), jnp.float32),
-        jax.ShapeDtypeStruct((PATCH, LANES), jnp.float32),
-        jax.ShapeDtypeStruct(bases, jnp.float32),
-    ]
-    out_specs = [vmem] * 3
+    if patch == 0:
+        shapes = [(RANK, PIXEL_ROWS * LANES), (RANK, LANES), (56, LANES), (RANK, frames)]
+    else:
+        shapes = [(RANK, PATCH, LANES), (PATCH, LANES), (2, RANK, frames)]
+    shapes = [jax.ShapeDtypeStruct(shape, jnp.float32) for shape in shapes]
+    out_specs = [vmem] * len(shapes)
     start = pltpu.VMEM((RANK, frames), jnp.float32)
     next_means = (16, LANES)
     if patch == 0:
@@ -523,12 +543,12 @@
             *(pltpu.VMEM(value.shape, jnp.float32) for value in operands[-3:]),
             *parts(PIXEL_ROWS, pltpu.VMEM),
         ]
-    scratch += [
-        pltpu.VMEM((56, LANES), jnp.float32),
-        pltpu.VMEM((RANK, PIXEL_ROWS * LANES), jnp.float32),
-        pltpu.VMEM((RANK * 48, LANES), jnp.float32),
-        pltpu.SemaphoreType.DMA((14,)),
-    ]
+        scratch += [
+            pltpu.VMEM((56, LANES), jnp.float32),
+            pltpu.VMEM((RANK, PIXEL_ROWS * LANES), jnp.float32),
+            pltpu.VMEM((RANK * 48, LANES), jnp.float32),
+        ]
+    scratch.append(pltpu.SemaphoreType.DMA((14,)))
     return pl.pallas_call(
         patch_1_kernel if patch else patch_0_kernel,
         out_shape=tuple(shapes),
@@ -560,8 +580,11 @@
     pairs = [(i, i ^ 1) for i in range(n_rows)]
     edge = lax.ppermute(first[:, : 2 * GROUP], "py", pairs)
     second = lax.all_to_all(second, ("px", "py"), split_axis=0, concat_axis=0, tiled=True)
-    *left, next_means, begin, next_movie, next_turned = decompose(0, place, first, edge, start)
+    projected, level, means, basis, next_means, begin, next_movie, next_turned = decompose(
+        0, place, first, edge, start
+    )
     begin = lax.ppermute(begin, "px", [(i, (i - 1) % n_cols) for i in range(n_cols)])
+    left = (*finish_0(place, projected, level, means), basis)
     spatial, background, bases = decompose(
         1, place, second, first, edge, begin, next_movie, next_turned, next_means, start, *left
     )

time: 114 us -> 114 us (level)
  waiting for transfers between devices: 39.5 us -> 37.7 us
  Pallas kernels: 48.6 us -> 50.2 us
    pallas_call x0 -> x1, Pallas kernels: none -> 2.2 us  [finish_0(): pl.pallas_call(finish_0_kernel, out_shape=(jax.ShapeDtypeStruct((RANK, PA...]
    ppermute x1, waiting for transfers between devices: 3.36 us -> 1.53 us  [on_device(): lax.ppermute(begin, 'px', [(i, (i - 1) % n_cols) for i in range(n_cols)])]
  transfers between devices with their start and end apart: 4 -> 4, of which waited for: 3 -> 3; matrix products, arithmetic and copies ran while one was open for 2% -> 2% of each run, Pallas kernels for 22% -> 24%
where the time goes in v7:
time: 114 us; the launch traced here: 113 us
  Pallas kernels  50.2 us (44%)
  waiting for transfers between devices  37.7 us (33%)
  starting transfers between devices  22 us (19%)
  local copies, waits for them, and re-layouts  1.95 us (2%)
    pallas_call x2, Pallas kernels, decompose(): pl.pallas_call(patch_1_kernel if patch else patch_0_kernel, out_shape=tup...  35.7 us
    all_to_all x1, waiting for transfers between devices, on_device(): lax.all_to_all(first, ('px', 'py'), split_axis=0, concat_axis=0, tiled=True)  33.8 us
    all_to_all x1, starting transfers between devices, on_device(): lax.all_to_all(first, ('px', 'py'), split_axis=0, concat_axis=0, tiled=True)  11.9 us
    pallas_call x2, Pallas kernels, spread(): pl.pallas_call(lambda *refs: spread_kernel(exchange, *refs), out_shape=ja...  10.5 us
    all_to_all x1, starting transfers between devices, on_device(): lax.all_to_all(second, ('px', 'py'), split_axis=0, concat_axis=0, tiled=T...  5.93 us
    ppermute x1, starting transfers between devices, on_device(): lax.ppermute(begin, 'px', [(i, (i - 1) % n_cols) for i in range(n_cols)])  2.97 us
    ppermute x1, waiting for transfers between devices, on_device(): edge = lax.ppermute(first[:, :2 * GROUP], 'py', pairs)  2.42 us
  transfers between devices with their start and end apart: 4, of which 3 were waited for; matrix products, arithmetic and copies ran while one was open for 2% of the time, Pallas kernels for 24%

profile of v7, /device:TPU:1, one launch (start us, length us, event | category | flops | bytes accessed | tf_op | source)
XLA Modules:
  0.0 113.2 jit_solution(9481330641905332799)
XLA Ops:
  0.6 6.0 %spread_0.1 = f32[8,16,48,128]{3,2,1,0:T(8,128)} custom-call(s32[1,2]{1,0:T(1,128)} %refs_0_.3, f32[1024,1024]{1,0:T(8,128)} %bitcast.9), custom_call_target="tpu_custom_call" | custom-call | tf_op jit(solution)/shard_map/spread_0/pallas_call | solution.py:144
  6.6 11.9 %all-to-all-start = ((f32[128,48,128]{2,1,0:T(8,128)}), f32[128,48,128]{2,1,0:T(8,128)}, u32[]{:S(2)}, u32[]{:S(2)}) async-start(f32[128,48,128]{2,1,0:T(8,128)} %bitcast.11), calls=%async_computation | async-start | bytes 6291456 | tf_op jit(solution)/shard_map/all_to_all | solution.py:576
  18.6 4.5 %spread_1.1 = f32[8,16,32,128]{3,2,1,0:T(8,128)} custom-call(s32[1,2]{1,0:T(1,128)} %refs_0_.3, f32[1024,1024]{1,0:T(8,128)} %bitcast.10), custom_call_target="tpu_custom_call" | custom-call | tf_op jit(solution)/shard_map/spread_1/pallas_call | solution.py:144
  23.1 1.8 %start_rows.1.start_ref = f32[16,128]{1,0:T(8,128)} custom-call(f32[16,128]{1,0:T(8,128)} %bitcast.13), custom_call_target="tpu_custom_call" | custom-call | tf_op jit(solution)/shard_map/start_rows/pallas_call | solution.py:242
  24.8 0.6 pad_add_fusion.place_ref
  25.4 33.8 %all-to-all-done.first_ref = f32[128,48,128]{2,1,0:T(8,128)} async-done(((f32[128,48,128]{2,1,0:T(8,128)}), f32[128,48,128]{2,1,0:T(8,128)}, u32[]{:S(2)}, u32[]{:S(2)}) %all-to-all-start) | async-done | bytes 3145760 | tf_op jit(solution)/shard_map/all_to_all | solution.py:576
  59.2 5.9 %all-to-all-start.1 = ((f32[128,32,128]{2,1,0:T(8,128)}), f32[128,32,128]{2,1,0:T(8,128)}, u32[]{:S(2)}, u32[]{:S(2)}) async-start(f32[128,32,128]{2,1,0:T(8,128)} %bitcast.12), calls=%async_computation.1 | async-start | bytes 4194304 | tf_op jit(solution)/shard_map/all_to_all | solution.py:582
  65.1 1.3 %slice.3 = f32[128,16,128]{2,1,0:T(8,128)S(1)} slice(f32[128,48,128]{2,1,0:T(8,128)} %all-to-all-done.first_ref), slice={[0:128], [0:16], [0:128]} | slice | bytes 2097152 | tf_op jit(solution)/shard_map/slice | solution.py:581
  66.4 1.2 %collective-permute-start = (f32[128,16,128]{2,1,0:T(8,128)S(1)}, f32[128,16,128]{2,1,0:T(8,128)}, u32[]{:S(2)}, u32[]{:S(2)}) collective-permute-start(f32[128,16,128]{2,1,0:T(8,128)S(1)} %slice.3), channel_id=1, source_target_pairs={{0,8},{8,0},{16,24},{24,16},{32,40},{40,32},{48,56},{56,48},{64,72... | collective-permute-start | bytes 3145736 | tf_op jit(solution)/shard_map/ppermute | solution.py:581
  67.7 2.4 %collective-permute-done.edge_ref = f32[128,16,128]{2,1,0:T(8,128)} collective-permute-done((f32[128,16,128]{2,1,0:T(8,128)S(1)}, f32[128,16,128]{2,1,0:T(8,128)}, u32[]{:S(2)}, u32[]{:S(2)}) %collective-permute-start) | collective-permute-done | bytes 1048608 | tf_op jit(solution)/shard_map/ppermute | solution.py:581
  70.1 18.2 %patch_0.1 = (f32[16,6400]{1,0:T(8,128)}, f32[16,128]{1,0:T(8,128)}, f32[56,128]{1,0:T(8,128)}, f32[16,128]{1,0:T(8,128)}, f32[16,128]{1,0:T(8,128)}, /*index=5*...) custom-call(s32[2]{0:T(128)} %pad_add_fusion.place_ref, f32[128,48,128]{2,1,0:T(8,128)} %all-to-all-done.first_ref, ...), custom_call_target="tpu_custom_call" | custom-call | flops 2726297600 | bytes 3276800 | tf_op jit(solution)/shard_map/patch_0/pallas_call | solution.py:552
  88.3 3.0 %collective-permute-start.1 = (f32[256,128]{1,0:T(8,128)}, f32[256,128]{1,0:T(8,128)S(1)}, u32[]{:S(2)}, u32[]{:S(2)}) collective-permute-start(f32[256,128]{1,0:T(8,128)} %get-tuple-element.24), channel_id=1, source_target_pairs={{0,7},{1,0},{2,1},{3,2},{4,3},{5,4},{6,5},{7,6},{8,15},{9,8},{10,9... | collective-permute-start | bytes 393224 | tf_op jit(solution)/shard_map/ppermute | solution.py:586
  91.3 2.2 %finish_0.1 = (f32[16,64,128]{2,1,0:T(8,128)}, f32[64,128]{1,0:T(8,128)}) custom-call(s32[2]{0:T(128)} %pad_add_fusion.place_ref, f32[16,6400]{1,0:T(8,128)} %get-tuple-element.28.projected, f32[16,128]{1,0:T(8,128)} %get-tuple-element.29.level, f32[56,128]{1,0:T(8,128)} %get-tuple-element.30.means), custom_call_target="tpu_custom_call" | custom-call | flops 16777216 | bytes 2097152 | tf_op jit(solution)/shard_map/finish_0/pallas_call | solution.py:367
  93.5 1.5 %collective-permute-done.1.begin_ref = f32[256,128]{1,0:T(8,128)S(1)} collective-permute-done((f32[256,128]{1,0:T(8,128)}, f32[256,128]{1,0:T(8,128)S(1)}, u32[]{:S(2)}, u32[]{:S(2)}) %collective-permute-start.1) | collective-permute-done | bytes 131104 | tf_op jit(solution)/shard_map/ppermute | solution.py:586
  95.0 0.0 copy-start
  95.0 0.0 all-to-all-done.1.second_ref
  95.0 0.6 copy-done
  95.7 17.5 %patch_1.1 = (f32[16,64,128]{2,1,0:T(8,128)}, f32[64,128]{1,0:T(8,128)}, f32[2,16,128]{2,1,0:T(8,128)}) custom-call(s32[2]{0:T(128)} %pad_add_fusion.place_ref, f32[128,32,128]{2,1,0:T(8,128)} %all-to-all-done.1.second_ref, f32[128,48,128]{2,1,0:T(8,128)} %all-to-all-done.first_ref, f32[128,16,128]{2,1,0:T(8,128)} %collective-permute-done.edge_ref, ...), custom_call_target="tpu_custom_call" | custom-call | flops 2726297600 | bytes 3276800 | tf_op jit(solution)/shard_map/patch_1/pallas_call | solution.py:552
Async XLA Ops:
  6.6 52.5 %all-to-all-start = ((f32[128,48,128]{2,1,0:T(8,128)}), f32[128,48,128]{2,1,0:T(8,128)}, u32[]{:S(2)}, u32[]{:S(2)}) async-start(f32[128,48,128]{2,1,0:T(8,128)} %bitcast.11), calls=%async_computation | async-start | bytes 6291456 | tf_op jit(solution)/shard_map/all_to_all | solution.py:576
  59.2 35.8 %all-to-all-start.1 = ((f32[128,32,128]{2,1,0:T(8,128)}), f32[128,32,128]{2,1,0:T(8,128)}, u32[]{:S(2)}, u32[]{:S(2)}) async-start(f32[128,32,128]{2,1,0:T(8,128)} %bitcast.12), calls=%async_computation.1 | async-start | bytes 4194304 | tf_op jit(solution)/shard_map/all_to_all | solution.py:582
  66.4 3.6 %collective-permute-start = (f32[128,16,128]{2,1,0:T(8,128)S(1)}, f32[128,16,128]{2,1,0:T(8,128)}, u32[]{:S(2)}, u32[]{:S(2)}) collective-permute-start(f32[128,16,128]{2,1,0:T(8,128)S(1)} %slice.3), channel_id=1, source_target_pairs={{0,8},{8,0},{16,24},{24,16},{32,40},{40,32},{48,56},{56,48},{64,72... | collective-permute-start | bytes 3145736 | tf_op jit(solution)/shard_map/ppermute | solution.py:581
  88.3 6.7 %collective-permute-start.1 = (f32[256,128]{1,0:T(8,128)}, f32[256,128]{1,0:T(8,128)S(1)}, u32[]{:S(2)}, u32[]{:S(2)}) collective-permute-start(f32[256,128]{1,0:T(8,128)} %get-tuple-element.24), channel_id=1, source_target_pairs={{0,7},{1,0},{2,1},{3,2},{4,3},{5,4},{6,5},{7,6},{8,15},{9,8},{10,9... | collective-permute-start | bytes 393224 | tf_op jit(solution)/shard_map/ppermute | solution.py:586
  95.0 0.6 copy-start
